TPU v7x, 256 devices: a whole 4x4x8 slice. The times are simulated.
256 devices in a mesh: row: 16 (over z, core), col: 8 (over x_hi, y), lrn: 2 (over x_lo).
Axes of the slice: x: 4 (x_hi: 2, x_lo: 2; x = x_hi * 2 + x_lo), y: 4, z: 8, core: 2. Of those that a mesh axis runs over, the one named last changes fastest.
Arguments:
- responses: int32 [4096, 16384], P('lrn', ('row', 'col')), may hold values 0 or 1
- observed: int32 [4096, 16384], P('lrn', ('row', 'col')), may hold values from 0 to 1, as said below
- qmatrix: int32 [16384, 8], P(('row', 'col')), may hold values from 0 to 1
- guess: float32 [16384], P(('row', 'col')), may hold values from 0.05 to 0.35
- slip: float32 [16384], P(('row', 'col')), may hold values from 0.05 to 0.35
Outputs:
- q3_scaled: float32 [16384, 16384], P('row', ('col', 'lrn'))
Inputs may be any that keep to these rules, and one draw needn't show every extreme that they name: Some items have no observed response from any learner.
All inputs are finite; a program needn't handle non-finite values. No bound on the sum of `responses` on one device may be relied on, other than what follows from the above.
Results may differ from a plain program's by a relative error of at most 0.008.
Values may be sent and summed in bfloat16 or wider, within the bound.
No kernel may reach another device: no remote copies, remote signals or barrier semaphores. Data moves between devices by JAX's collectives and lax.ppermute only.
A program may use at most 128 MiB of HBM per device.

v0:
```python
import jax
import jax.numpy as jnp
from jax import lax
from jax.sharding import PartitionSpec as P

ATTRS = 8
PROFILES = 256


def spread(x, axis, root):
    mine = lax.axis_index(axis) == root
    return lax.psum(jnp.where(mine, x, jnp.zeros_like(x)), axis)


def success(qmatrix, guess, slip):
    codes = jnp.arange(PROFILES, dtype=jnp.int32)
    powers = jnp.arange(ATTRS, dtype=jnp.int32)
    bits = (codes[None, :] >> powers[:, None] & 1).astype(jnp.float32)
    lacking = jnp.dot(qmatrix.astype(jnp.float32), 1.0 - bits, precision=lax.Precision.HIGHEST)
    return jnp.where(lacking == 0.0, 1.0 - slip[:, None], guess[:, None])


def learner_product(left, right):
    return lax.dot_general(
        left, right, (((0,), (0,)), ((), ())), preferred_element_type=jnp.float32
    )


def shards(responses, observed, qmatrix, guess, slip):
    prob = success(qmatrix, guess, slip)
    answered = responses.astype(jnp.float32)
    seen = observed.astype(jnp.float32)
    partial_value = jnp.dot(seen * answered, jnp.log(prob), precision=lax.Precision.HIGHEST)
    partial_value = partial_value + jnp.dot(
        seen * (1.0 - answered), jnp.log(1.0 - prob), precision=lax.Precision.HIGHEST
    )
    loglik = lax.psum(partial_value, ("row", "col"))
    posterior = jax.nn.softmax(loglik, axis=1).astype(jnp.bfloat16)
    expected = jnp.dot(posterior, prob.astype(jnp.bfloat16).T, preferred_element_type=jnp.float32)
    resid = seen * (answered - expected)
    count, total, square = lax.psum(
        (jnp.sum(seen, axis=0), jnp.sum(resid, axis=0), jnp.sum(resid * resid, axis=0)), "lrn"
    )
    count = jnp.maximum(count, 1.0)
    mean = total / count
    var = square / count - mean * mean
    zres = (seen * (resid - mean) * lax.rsqrt(var + 1e-06) * lax.rsqrt(count)).astype(jnp.bfloat16)
    panel = lax.all_gather(zres, "col", axis=1, tiled=True)
    learner_total = zres.shape[0] * lax.axis_size("lrn")
    whole_panel = lax.all_gather(panel, "lrn", axis=0, tiled=True)
    repeats = lax.axis_size("row") // (lax.axis_size("col") * lax.axis_size("lrn"))
    tile_index = lax.axis_index("col") * lax.axis_size("lrn") + lax.axis_index("lrn")
    pieces = spread(whole_panel, "row", tile_index * repeats + 0)
    gram = learner_product(whole_panel, pieces)
    return gram * jnp.sqrt(jnp.float32(learner_total))


def solution(mesh):
    placed = (
        P("lrn", ("row", "col")),
        P("lrn", ("row", "col")),
        P(("row", "col"), None),
        P(("row", "col")),
        P(("row", "col")),
    )
    return jax.shard_map(
        shards, mesh=mesh, in_specs=placed, out_specs=P("row", ("col", "lrn")), check_vma=False
    )
```

profile of v0, /device:TPU:24, one launch (start us, length us, event | category | flops | bytes accessed | tf_op | source)
XLA Modules:
  0.0 1651.9 jit_solution(6100974589586948307)
XLA Ops:
  6.5 0.0 copy-start
  6.5 0.0 copy-start.1
  6.5 0.0 all-reduce.4.cloned.1.call-start
  6.5 0.8 broadcast_subtract_fusion
  7.3 1.1 fusion
  8.4 0.0 copy-start.2
  8.5 3.4 fusion.3
  11.9 0.0 copy-done
  11.9 0.0 copy-done.1
  11.9 3.2 convolution_add_fusion
  15.1 0.0 copy-done.2
  15.1 0.0 all-reduce.4.cloned.1.call-update
  15.1 0.0 all-gather.3.cloned.1.call-start
  15.1 1275.0 %all-reduce.4.cloned.1.call-done = f32[2048,256]{1,0:T(8,128)} async-done(((f32[2048,256]{1,0:T(8,128)}), f32[2048,256]{1,0:T(8,128)}) %all-reduce.4.cloned.1.call-update) | async-done | bytes 2097168 | tf_op jit(solution)/shard_map/psum | solution.py:37
  1290.1 3.9 online-softmax
  1294.0 1.5 multiply_reduce_fusion
  1295.5 4.9 all-reduce
  1300.5 1.0 multiply_convert_fusion
  1301.5 0.0 all-gather.3.cloned.1.call-update
  1301.5 0.0 all-gather.5.cloned.1.call-start
  1301.6 76.0 %all-gather.3.cloned.1.call-done = bf16[2048,1024]{1,0:T(8,128)(2,1)} async-done(((bf16[2048,128]{1,0:T(8,128)(2,1)}), bf16[2048,1024]{1,0:T(8,128)(2,1)}) %all-gather.3.cloned.1.call-update) | async-done | bytes 4194320 | tf_op jit(solution)/shard_map/all_gather | solution.py:48
  1377.6 0.0 all-gather.5.cloned.1.call-update
  1377.6 0.0 all-reduce.6.cloned.1.call-start
  1377.6 110.8 %all-gather.5.cloned.1.call-done = bf16[4096,1024]{1,0:T(8,128)(2,1)} async-done(((bf16[2048,1024]{1,0:T(8,128)(2,1)}), bf16[4096,1024]{1,0:T(8,128)(2,1)}) %all-gather.5.cloned.1.call-update) | async-done | bytes 8388624 | tf_op jit(solution)/shard_map/all_gather | solution.py:50
  1488.5 3.8 broadcast_select_fusion
  1492.3 0.0 all-reduce.6.cloned.1.call-update
  1492.3 138.1 %all-reduce.6.cloned.1.call-done = bf16[4096,1024]{1,0:T(8,128)(2,1)} async-done(((bf16[4096,1024]{1,0:T(8,128)(2,1)}), bf16[4096,1024]{1,0:T(8,128)(2,1)}) %all-reduce.6.cloned.1.call-update) | async-done | bytes 8388624 | tf_op jit(solution)/shard_map/psum | solution.py:12
  1630.4 15.0 convolution_multiply_fusion
  (1 shorter events, 0.0 us)
Async XLA Ops:
  6.5 5.3 copy-start
  6.5 5.4 copy-start.1
  6.5 1283.6 %all-reduce.4.cloned.1.call-start = ((), (), s32[]{:S(2)}) async-start(), calls=%async_computation | async-start | bytes 4194304 | tf_op jit(solution)/shard_map/psum | solution.py:37
  8.4 6.6 copy-start.2
  15.1 1362.5 %all-gather.3.cloned.1.call-start = ((), (), s32[]{:S(2)}) async-start(), calls=%async_computation.1 | async-start | bytes 4718592 | tf_op jit(solution)/shard_map/all_gather | solution.py:48
  1301.5 187.0 %all-gather.5.cloned.1.call-start = ((), (), s32[]{:S(2)}) async-start(), calls=%async_computation.2 | async-start | bytes 12582912 | tf_op jit(solution)/shard_map/all_gather | solution.py:50
  1377.6 252.8 %all-reduce.6.cloned.1.call-start = ((), (), s32[]{:S(2)}) async-start(), calls=%async_computation.3 | async-start | bytes 16777216 | tf_op jit(solution)/shard_map/psum | solution.py:12
Sparse Core Ops, SparseCore 0:
  15.2 1274.8 all-reduce.3
  1301.6 75.8 all-gather.2
  1379.5 108.9 all-gather.4
  1492.4 137.9 all-reduce.5
where the time goes:
time: 1650 us
  waiting for transfers between devices  1600 us (97%)
  matrix products  22.7 us (1%)
    psum x1, waiting for transfers between devices, shards(): loglik = lax.psum(partial_value, ('row', 'col'))  1270 us
    psum x1, waiting for transfers between devices, spread(): return lax.psum(jnp.where(mine, x, jnp.zeros_like(x)), axis)  138 us
    all_gather x1, waiting for transfers between devices, shards(): whole_panel = lax.all_gather(panel, 'lrn', axis=0, tiled=True)  111 us
    all_gather x1, waiting for transfers between devices, shards(): panel = lax.all_gather(zres, 'col', axis=1, tiled=True)  76 us
  transfers between devices with their start and end apart: 4, of which 4 were waited for; matrix products, arithmetic and copies ran while one was open for 0% of the time, Pallas kernels for 0%

commit v1 on v0

v1 whole, which is shorter than its diff:
```python
import jax
import jax.numpy as jnp
from jax import lax
from jax.sharding import Mesh, PartitionSpec as P

ATTRS = 8
PROFILES = 256

ROW = ("z", "k")
COL = ("xh", "y")
PLANE = ("xh", "y", "xl")
X = ("xh", "xl")


def shift(x, axis, n, by):
    return lax.ppermute(x, axis, [(i, (i + by) % n) for i in range(n)])


def triple(x):
    high = lax.reduce_precision(x, 8, 7)
    rest = x - high
    middle = lax.reduce_precision(rest, 8, 7)
    return high, middle, rest - middle


def ring(x, axis):
    half = x.shape[0] // 2
    before = shift(x, axis, 4, 1)
    after = shift(x, axis, 4, -1)
    low = shift(before[:half], axis, 4, 1)
    high = shift(after[half:], axis, 4, -1)
    return before, after, low, high


def place(panel, block, start):
    return lax.dynamic_update_slice(panel, block, [jnp.int32(s) for s in start])


def spread_plane(z):
    chunks, rows, items = z.shape
    half = chunks // 2
    x, y = lax.axis_index(X), lax.axis_index("y")
    panel = jnp.zeros((chunks, 4, 4, rows, items), z.dtype)

    line = jnp.zeros((half, 4, rows, items), z.dtype)
    mine = z[:half]
    before, after, low, high = ring(mine, X)
    line = place(line, mine[:, None], (0, x, 0, 0))
    line = place(line, before[:, None], (0, (x + 3) % 4, 0, 0))
    line = place(line, after[:, None], (0, (x + 1) % 4, 0, 0))
    line = place(line, low[:, None], (0, (x + 2) % 4, 0, 0))
    line = place(line, high[:, None], (half // 2, (x + 2) % 4, 0, 0))
    tall = jnp.zeros((half, 4, rows, items), z.dtype)
    mine = z[half:]
    before, after, low, high = ring(mine, "y")
    tall = place(tall, mine[:, None], (0, y, 0, 0))
    tall = place(tall, before[:, None], (0, (y + 3) % 4, 0, 0))
    tall = place(tall, after[:, None], (0, (y + 1) % 4, 0, 0))
    tall = place(tall, low[:, None], (0, (y + 2) % 4, 0, 0))
    tall = place(tall, high[:, None], (half // 2, (y + 2) % 4, 0, 0))

    before, after, low, high = ring(line, "y")
    panel = place(panel, line[:, None], (0, y, 0, 0, 0))
    panel = place(panel, before[:, None], (0, (y + 3) % 4, 0, 0, 0))
    panel = place(panel, after[:, None], (0, (y + 1) % 4, 0, 0, 0))
    panel = place(panel, low[:, None], (0, (y + 2) % 4, 0, 0, 0))
    panel = place(panel, high[:, None], (half // 2, (y + 2) % 4, 0, 0, 0))
    before, after, low, high = ring(tall, X)
    panel = place(panel, tall[:, :, None], (half, 0, x, 0, 0))
    panel = place(panel, before[:, :, None], (half, 0, (x + 3) % 4, 0, 0))
    panel = place(panel, after[:, :, None], (half, 0, (x + 1) % 4, 0, 0))
    panel = place(panel, low[:, :, None], (half, 0, (x + 2) % 4, 0, 0))
    panel = place(panel, high[:, :, None], (half + half // 2, 0, (x + 2) % 4, 0, 0))
    return panel


def swap(x, axis):
    return lax.all_to_all(x, axis, 0, 0, tiled=True)


def shards(responses, observed, qmatrix, guess, slip):
    learners, items = responses.shape
    cols, rows = 8, 16
    part = learners // cols
    chunk = part // rows

    right = (responses * observed).astype(jnp.bfloat16).reshape(cols, part, items)
    seen = observed.astype(jnp.bfloat16).reshape(cols, part, items)
    table = jnp.concatenate(
        [qmatrix.astype(jnp.float32).T, jnp.stack(triple(guess) + triple(slip)), jnp.zeros((2, items))]
    ).astype(jnp.bfloat16)
    table = jnp.broadcast_to(table, (cols,) + table.shape)
    mixed = swap(jnp.concatenate([right, seen, table], axis=1), COL)
    mixed = mixed.transpose(1, 0, 2).reshape(2 * part + 16, cols * items)
    right, seen, table = mixed[:part], mixed[part : 2 * part], mixed[2 * part :].astype(jnp.float32)
    needs = table[:ATTRS]
    guess = table[8] + table[9] + table[10]
    slip = table[11] + table[12] + table[13]

    codes = jnp.arange(PROFILES, dtype=jnp.int32)
    powers = jnp.arange(ATTRS, dtype=jnp.int32)
    bits = (codes[:, None] >> powers[None, :] & 1).astype(jnp.float32)
    lacking = jnp.dot(1.0 - bits, needs, precision=lax.Precision.HIGHEST)
    prob = jnp.where(lacking == 0.0, 1.0 - slip, guess)
    log0 = jnp.log(1.0 - prob)
    weights = jnp.concatenate([jnp.log(prob) - log0, log0], axis=1)
    data = jnp.concatenate([right, seen], axis=1)
    loglik = sum(
        lax.dot_general(data, w.astype(jnp.bfloat16), (((1,), (1,)), ((), ())), preferred_element_type=jnp.float32)
        for w in triple(weights)
    )
    loglik = jnp.sum(swap(loglik, ROW).reshape(rows, chunk, PROFILES), axis=0)
    posterior = jax.nn.softmax(loglik, axis=1).astype(jnp.bfloat16)
    posterior = swap(jnp.broadcast_to(posterior, (rows, chunk, PROFILES)), ROW).reshape(part, PROFILES)

    expected = jnp.dot(posterior, prob.astype(jnp.bfloat16), preferred_element_type=jnp.float32)
    seen = seen.astype(jnp.float32)
    resid = right.astype(jnp.float32) - seen * expected
    sums = jnp.stack([jnp.sum(seen, axis=0), jnp.sum(resid, axis=0), jnp.sum(resid * resid, axis=0)])
    sums = jnp.sum(swap(jnp.broadcast_to(sums, (16,) + sums.shape), PLANE), axis=0)
    count = jnp.maximum(sums[0], 1.0)
    mean = sums[1] / count
    var = sums[2] / count - mean * mean
    root = jnp.sqrt(jnp.sqrt(jnp.float32(learners * 2)))
    zres = (seen * (resid - mean) * (lax.rsqrt(var + 1e-06) * lax.rsqrt(count) * root)).astype(jnp.bfloat16)

    zres = zres.reshape(rows, chunk, cols * items)
    turned = swap(swap(zres, ROW), PLANE)
    turned = turned.reshape(2, 4, 2, chunk, cols * items).transpose(1, 0, 2, 3, 4)
    columns = lax.all_gather(turned, ROW)
    panel = spread_plane(zres)
    flat = (rows * 16 * chunk, cols * items)
    return lax.dot_general(
        panel.reshape(flat), columns.reshape(flat), (((0,), (0,)), ((), ())), preferred_element_type=jnp.float32
    )


def solution(mesh):
    named = Mesh(mesh.devices.reshape(8, 2, 2, 4, 2), ("z", "k", "xh", "y", "xl"))
    items = ROW + COL
    placed = (P("xl", items), P("xl", items), P(items, None), P(items), P(items))
    return jax.shard_map(shards, mesh=named, in_specs=placed, out_specs=P(ROW, PLANE), check_vma=False)
```

time: 1650 us -> 213 us (0.13)
  waiting for transfers between devices: 1600 us -> 32.2 us
  blocking collectives: 4.94 us -> 88.8 us
  starting transfers between devices: 0.12 us -> 29.9 us
  local copies, waits for them, and re-layouts: 0.01 us -> 24.5 us
    psum x2 -> x0, waiting for transfers between devices: 1410 us -> none  [the longest x1 1270 us: shards(): loglik = lax.psum(partial_value, ('row', 'col'))]
    all_gather x2 -> x1, waiting for transfers between devices: 187 us -> 0.01 us  [shards(): columns = lax.all_gather(turned, ROW)]
    all_to_all x0 -> x5, blocking collectives: none -> 88.8 us  [swap(): return lax.all_to_all(x, axis, 0, 0, tiled=True)]
    ppermute x0 -> x16, starting transfers between devices: none -> 26.4 us  [shift(): return lax.ppermute(x, axis, [(i, (i + by) % n) for i in range(n)])]
    ppermute x0 -> x16, waiting for transfers between devices: none -> 23.6 us  [shift(): return lax.ppermute(x, axis, [(i, (i + by) % n) for i in range(n)])]
  transfers between devices with their start and end apart: 4 -> 18, of which waited for: 4 -> 6; matrix products, arithmetic and copies ran while one was open for 0% -> 7% of each run, Pallas kernels for 0% -> 0%
where the time goes in v1:
time: 213 us; the launch traced here: 211 us
  blocking collectives  88.8 us (42%)
  waiting for transfers between devices  32.2 us (15%)
  starting transfers between devices  29.9 us (14%)
  local copies, waits for them, and re-layouts  24.5 us (12%)
  matrix products  17.9 us (8%)
  between operations  13.8 us (6%)
  other arithmetic  4.25 us (2%)
    all_to_all x5, blocking collectives, swap(): return lax.all_to_all(x, axis, 0, 0, tiled=True)  88.8 us
    ppermute x16, starting transfers between devices, shift(): return lax.ppermute(x, axis, [(i, (i + by) % n) for i in range(n)])  26.4 us
    ppermute x16, waiting for transfers between devices, shift(): return lax.ppermute(x, axis, [(i, (i + by) % n) for i in range(n)])  23.6 us
    dot_general x1, matrix products, shards(): lax.dot_general(panel.reshape(flat), columns.reshape(flat), (((0,), (0,))...  15 us
    dynamic_update_slice x20, local copies, waits for them, and re-layouts, place(): return lax.dynamic_update_slice(panel, block, [jnp.int32(s) for s in start])  10.2 us
    all_to_all x1, waiting for transfers between devices, swap(): return lax.all_to_all(x, axis, 0, 0, tiled=True)  8.55 us
    all_gather x1, local copies, waits for them, and re-layouts, shards(): columns = lax.all_gather(turned, ROW)  8.54 us
    broadcast_in_dim x1, local copies, waits for them, and re-layouts, spread_plane(): panel = jnp.zeros((chunks, 4, 4, rows, items), z.dtype)  4.3 us
  transfers between devices with their start and end apart: 18, of which 6 were waited for; matrix products, arithmetic and copies ran while one was open for 7% of the time, Pallas kernels for 0%

profile of v1, /device:TPU:24, one launch (start us, length us, event | category | flops | bytes accessed | tf_op | source)
XLA Modules:
  0.0 211.3 jit_solution(15808034937467861891)
XLA Ops:
  7.9 2.0 multiply_convert_fusion
  10.1 22.6 %all_to_all.34 = bf16[8,528,128]{2,1,0:T(8,128)(2,1)S(1)} all-to-all(bf16[8,528,128]{2,1,0:T(8,128)(2,1)S(1)} %pad_maximum_fusion.1), channel_id=1, replica_groups=mesh['z'=8,'k'=2,'xh'=2,'y'=4,'xl'=2] {'xh','y'}, dimensions={0} | all-to-all | bytes 2162688 | tf_op jit(solution)/shard_map/all_to_all | solution.py:78
  32.9 0.9 fusion.4
  35.4 19.6 %all_to_all.35 = f32[16,16,256]{2,1,0:T(8,128)S(1)} all-to-all(f32[16,16,256]{2,1,0:T(8,128)S(1)} %bitcast.143), channel_id=1, replica_groups=mesh['z'=8,'k'=2,'xh'=2,'y'=4,'xl'=2] {'z','k'}, dimensions={0} | all-to-all | bytes 524288 | tf_op jit(solution)/shard_map/all_to_all | solution.py:78
  56.1 3.5 %all-to-all-start.2 = ((bf16[16,16,256]{2,1,0:T(8,128)(2,1)}), bf16[16,16,256]{2,1,0:T(8,128)(2,1)S(1)}, u32[]{:S(2)}, u32[]{:S(2)}) async-start(bf16[16,16,256]{2,1,0:T(8,128)(2,1)} %broadcast_in_dim.94), calls=%async_computation.2 | async-start | bytes 262144 | tf_op jit(solution)/shard_map/all_to_all | solution.py:78
  59.7 8.5 %all-to-all-done.2 = bf16[16,16,256]{2,1,0:T(8,128)(2,1)S(1)} async-done(((bf16[16,16,256]{2,1,0:T(8,128)(2,1)}), bf16[16,16,256]{2,1,0:T(8,128)(2,1)S(1)}, u32[]{:S(2)}, u32[]{:S(2)}) %all-to-all-start.2) | async-done | bytes 131104 | tf_op jit(solution)/shard_map/all_to_all | solution.py:78
  68.8 12.2 %all_to_all.36 = f32[16,3,1024]{2,1,0:T(4,128)S(1)} all-to-all(f32[16,3,1024]{2,1,0:T(4,128)S(1)} %broadcast_in_dim.95), channel_id=1, replica_groups=mesh['z'=8,'k'=2,'xh'=2,'y'=4,'xl'=2] {'xh','y','xl'}, dimensions={0} | all-to-all | bytes 393216 | tf_op jit(solution)/shard_map/all_to_all | solution.py:78
  81.3 18.6 %all_to_all.37 = bf16[16,16,1024]{2,1,0:T(8,128)(2,1)S(1)} all-to-all(bf16[16,16,1024]{2,1,0:T(8,128)(2,1)S(1)} %bitcast.133), channel_id=1, replica_groups=mesh['z'=8,'k'=2,'xh'=2,'y'=4,'xl'=2] {'z','k'}, dimensions={0} | all-to-all | bytes 1048576 | tf_op jit(solution)/shard_map/all_to_all | solution.py:78
  99.9 15.8 %all_to_all.38 = bf16[16,16,1024]{2,1,0:T(8,128)(2,1)} all-to-all(bf16[16,16,1024]{2,1,0:T(8,128)(2,1)S(1)} %all_to_all.37), channel_id=1, replica_groups=mesh['z'=8,'k'=2,'xh'=2,'y'=4,'xl'=2] {'xh','y','xl'}, dimensions={0} | all-to-all | bytes 1048576 | tf_op jit(solution)/shard_map/all_to_all | solution.py:78
  115.8 1.8 collective-permute-start.8
  118.4 2.8 %collective-permute-start.1 = (bf16[8,16,1024]{2,1,0:T(8,128)(2,1)S(1)}, bf16[8,16,1024]{2,1,0:T(8,128)(2,1)S(1)}, u32[]{:S(2)}, u32[]{:S(2)}) collective-permute-start(bf16[8,16,1024]{2,1,0:T(8,128)(2,1)S(1)} %bitcast.138), channel_id=1, source_target_pairs={{0,9},{1,0},{8,1},{9,8},{2,11},{3,2},{10,3},{11,10},{4,13},{5,4},{... | collective-permute-start | bytes 786440 | tf_op jit(solution)/shard_map/ppermute | solution.py:16
  121.4 2.8 %collective-permute-done.8 = bf16[8,16,1024]{2,1,0:T(8,128)(2,1)S(1)} collective-permute-done((bf16[8,16,1024]{2,1,0:T(8,128)(2,1)S(1)}, bf16[8,16,1024]{2,1,0:T(8,128)(2,1)S(1)}, u32[]{:S(2)}, u32[]{:S(2)}) %collective-permute-start.8) | collective-permute-done | bytes 262176 | tf_op jit(solution)/shard_map/ppermute | solution.py:16
  124.3 3.4 %collective-permute-start.10 = (bf16[4,16,1024]{2,1,0:T(8,128)(2,1)S(1)}, bf16[4,16,1024]{2,1,0:T(8,128)(2,1)S(1)}, u32[]{:S(2)}, u32[]{:S(2)}) collective-permute-start(bf16[4,16,1024]{2,1,0:T(8,128)(2,1)S(1)} %slice.139), channel_id=1, source_target_pairs={{0,2},{2,4},{4,6},{6,0},{1,3},{3,5},{5,7},{7,1},{8,10},{10,12},{12... | collective-permute-start | bytes 393224 | tf_op jit(solution)/shard_map/ppermute | solution.py:16
  128.5 2.7 %collective-permute-start.3 = (bf16[4,16,1024]{2,1,0:T(8,128)(2,1)S(1)}, bf16[4,16,1024]{2,1,0:T(8,128)(2,1)S(1)}, u32[]{:S(2)}, u32[]{:S(2)}) collective-permute-start(bf16[4,16,1024]{2,1,0:T(8,128)(2,1)S(1)} %slice.135), channel_id=1, source_target_pairs={{0,9},{1,0},{8,1},{9,8},{2,11},{3,2},{10,3},{11,10},{4,13},{5,4},{... | collective-permute-start | bytes 393224 | tf_op jit(solution)/shard_map/ppermute | solution.py:16
  131.3 2.7 %collective-permute-done.2 = bf16[4,16,1024]{2,1,0:T(8,128)(2,1)S(1)} collective-permute-done((bf16[4,16,1024]{2,1,0:T(8,128)(2,1)S(1)}, bf16[4,16,1024]{2,1,0:T(8,128)(2,1)S(1)}, u32[]{:S(2)}, u32[]{:S(2)}) %collective-permute-start.2) | collective-permute-done | bytes 131104 | tf_op jit(solution)/shard_map/ppermute | solution.py:16
  134.1 3.5 %collective-permute-start.4 = (bf16[8,4,16,1024]{3,2,1,0:T(8,128)(2,1)S(1)}, bf16[8,4,16,1024]{3,2,1,0:T(8,128)(2,1)S(1)}, u32[]{:S(2)}, u32[]{:S(2)}) collective-permute-start(bf16[8,4,16,1024]{3,2,1,0:T(8,128)(2,1)S(1)} %bitcast_dynamic-update-slice_fusion.19), channel_id=1, source_target_pairs={{0,2},{2,4},{4,6},{6,0},{1,3},{3,5},{5,7},{7,1},{8,10},{10,12},{12... | collective-permute-start | bytes 3145736 | tf_op jit(solution)/shard_map/ppermute | solution.py:16
  137.7 3.4 %collective-permute-start.13 = (bf16[8,4,16,1024]{3,2,1,0:T(8,128)(2,1)S(1)}, bf16[8,4,16,1024]{3,2,1,0:T(8,128)(2,1)S(1)}, u32[]{:S(2)}, u32[]{:S(2)}) collective-permute-start(bf16[8,4,16,1024]{3,2,1,0:T(8,128)(2,1)S(1)} %bitcast_dynamic-update-slice_fusion.18), channel_id=1, source_target_pairs={{0,9},{1,0},{8,1},{9,8},{2,11},{3,2},{10,3},{11,10},{4,13},{5,4},{... | collective-permute-start | bytes 3145736 | tf_op jit(solution)/shard_map/ppermute | solution.py:16
  141.1 4.3 %broadcast_in_dim.89 = bf16[16,4,4,16,1024]{4,3,2,1,0:T(8,128)(2,1)} broadcast(bf16[]{:T(256)} %constant.79.clone.1), dimensions={} | broadcast | bytes 8388610 | tf_op jit(solution)/shard_map/broadcast_in_dim | solution.py:43
  145.4 1.1 bitcast_dynamic-update-slice_fusion.5
  146.5 12.2 %collective-permute-done.4 = bf16[8,4,16,1024]{3,2,1,0:T(8,128)(2,1)S(1)} collective-permute-done((bf16[8,4,16,1024]{3,2,1,0:T(8,128)(2,1)S(1)}, bf16[8,4,16,1024]{3,2,1,0:T(8,128)(2,1)S(1)}, u32[]{:S(2)}, u32[]{:S(2)}) %collective-permute-start.4) | collective-permute-done | bytes 1048608 | tf_op jit(solution)/shard_map/ppermute | solution.py:16
  158.7 3.8 %collective-permute-start.6 = (bf16[4,4,16,1024]{3,2,1,0:T(8,128)(2,1)S(1)}, bf16[4,4,16,1024]{3,2,1,0:T(8,128)(2,1)S(1)}, u32[]{:S(2)}, u32[]{:S(2)}) collective-permute-start(bf16[4,4,16,1024]{3,2,1,0:T(8,128)(2,1)S(1)} %slice.136), channel_id=1, source_target_pairs={{0,2},{2,4},{4,6},{6,0},{1,3},{3,5},{5,7},{7,1},{8,10},{10,12},{12... | collective-permute-start | bytes 1572872 | tf_op jit(solution)/shard_map/ppermute | solution.py:16
  162.8 3.3 %collective-permute-start.15 = (bf16[4,4,16,1024]{3,2,1,0:T(8,128)(2,1)S(1)}, bf16[4,4,16,1024]{3,2,1,0:T(8,128)(2,1)S(1)}, u32[]{:S(2)}, u32[]{:S(2)}) collective-permute-start(bf16[4,4,16,1024]{3,2,1,0:T(8,128)(2,1)S(1)} %slice.142), channel_id=1, source_target_pairs={{0,9},{1,0},{8,1},{9,8},{2,11},{3,2},{10,3},{11,10},{4,13},{5,4},{... | collective-permute-start | bytes 1572872 | tf_op jit(solution)/shard_map/ppermute | solution.py:16
  166.1 1.1 bitcast_dynamic-update-slice_fusion.4
  167.2 1.1 bitcast_dynamic-update-slice_fusion.3
  168.2 3.2 %collective-permute-done.6 = bf16[4,4,16,1024]{3,2,1,0:T(8,128)(2,1)S(1)} collective-permute-done((bf16[4,4,16,1024]{3,2,1,0:T(8,128)(2,1)S(1)}, bf16[4,4,16,1024]{3,2,1,0:T(8,128)(2,1)S(1)}, u32[]{:S(2)}, u32[]{:S(2)}) %collective-permute-start.6) | collective-permute-done | bytes 524320 | tf_op jit(solution)/shard_map/ppermute | solution.py:16
  172.3 2.7 %collective-permute-done.7 = bf16[4,4,16,1024]{3,2,1,0:T(8,128)(2,1)S(1)} collective-permute-done((bf16[4,4,16,1024]{3,2,1,0:T(8,128)(2,1)S(1)}, bf16[4,4,16,1024]{3,2,1,0:T(8,128)(2,1)S(1)}, u32[]{:S(2)}, u32[]{:S(2)}) %collective-permute-start.7) | collective-permute-done | bytes 524320 | tf_op jit(solution)/shard_map/ppermute | solution.py:16
  175.8 1.1 bitcast_dynamic-update-slice_fusion.2
  176.9 1.1 bitcast_dynamic-update-slice_fusion.1
  178.0 1.1 bitcast_dynamic-update-slice_fusion
  180.0 0.9 bitcast_dynamic-update-slice_fusion.11
  180.9 8.5 %copy.112 = bf16[64,2,2,16,1024]{4,3,2,1,0:T(8,128)(2,1)} copy(bf16[64,2,2,16,1024]{4,3,2,0,1:T(8,128)(2,1)} %all-gather.3.cloned.1.call-done) | data formatting | bytes 16777216 | tf_op jit(solution)/shard_map/all_gather | solution.py:130
  189.5 15.0 %fusion.37 = f32[1024,1024]{1,0:T(8,128)} fusion(bf16[4096,1024]{1,0:T(8,128)(2,1)} %bitcast.59, bf16[4096,1024]{1,0:T(8,128)(2,1)} %bitcast.128), kind=kOutput, calls=%fused_computation.99 | convolution fusion | flops 8589934592 | bytes 20971520 | tf_op jit(solution)/shard_map/dot_general | solution.py:133
  (72 shorter events, 10.2 us)
Async XLA Ops:
  56.1 12.2 %all-to-all-start.2 = ((bf16[16,16,256]{2,1,0:T(8,128)(2,1)}), bf16[16,16,256]{2,1,0:T(8,128)(2,1)S(1)}, u32[]{:S(2)}, u32[]{:S(2)}) async-start(bf16[16,16,256]{2,1,0:T(8,128)(2,1)} %broadcast_in_dim.94), calls=%async_computation.2 | async-start | bytes 262144 | tf_op jit(solution)/shard_map/all_to_all | solution.py:78
  59.6 121.3 %all-gather.3.cloned.1.call-start = ((), (), s32[]{:S(2)}) async-start(), calls=%async_computation.6 | async-start | bytes 8912896 | tf_op jit(solution)/shard_map/all_gather | solution.py:130
  115.8 8.5 %collective-permute-start.8 = (bf16[8,16,1024]{2,1,0:T(8,128)(2,1)S(1)}, bf16[8,16,1024]{2,1,0:T(8,128)(2,1)S(1)}, u32[]{:S(2)}, u32[]{:S(2)}) collective-permute-start(bf16[8,16,1024]{2,1,0:T(8,128)(2,1)S(1)} %bitcast.140), channel_id=1, source_target_pairs={{0,2},{2,4},{4,6},{6,0},{1,3},{3,5},{5,7},{7,1},{8,10},{10,12},{12... | collective-permute-start | bytes 786440 | tf_op jit(solution)/shard_map/ppermute | solution.py:16
  117.6 10.1 %collective-permute-start.9 = (bf16[8,16,1024]{2,1,0:T(8,128)(2,1)S(1)}, bf16[8,16,1024]{2,1,0:T(8,128)(2,1)S(1)}, u32[]{:S(2)}, u32[]{:S(2)}) collective-permute-start(bf16[8,16,1024]{2,1,0:T(8,128)(2,1)S(1)} %bitcast.141), channel_id=1, source_target_pairs={{0,6},{2,0},{4,2},{6,4},{1,7},{3,1},{5,3},{7,5},{8,14},{10,8},{12,... | collective-permute-start | bytes 786440 | tf_op jit(solution)/shard_map/ppermute | solution.py:16
  117.9 9.9 %collective-permute-start = (bf16[8,16,1024]{2,1,0:T(8,128)(2,1)S(1)}, bf16[8,16,1024]{2,1,0:T(8,128)(2,1)S(1)}, u32[]{:S(2)}, u32[]{:S(2)}) collective-permute-start(bf16[8,16,1024]{2,1,0:T(8,128)(2,1)S(1)} %bitcast.137), channel_id=1, source_target_pairs={{0,1},{1,8},{8,9},{9,0},{2,3},{3,10},{10,11},{11,2},{4,5},{5,12},{... | collective-permute-start | bytes 786440 | tf_op jit(solution)/shard_map/ppermute | solution.py:16
  118.4 10.1 %collective-permute-start.1 = (bf16[8,16,1024]{2,1,0:T(8,128)(2,1)S(1)}, bf16[8,16,1024]{2,1,0:T(8,128)(2,1)S(1)}, u32[]{:S(2)}, u32[]{:S(2)}) collective-permute-start(bf16[8,16,1024]{2,1,0:T(8,128)(2,1)S(1)} %bitcast.138), channel_id=1, source_target_pairs={{0,9},{1,0},{8,1},{9,8},{2,11},{3,2},{10,3},{11,10},{4,13},{5,4},{... | collective-permute-start | bytes 786440 | tf_op jit(solution)/shard_map/ppermute | solution.py:16
  124.3 13.3 %collective-permute-start.10 = (bf16[4,16,1024]{2,1,0:T(8,128)(2,1)S(1)}, bf16[4,16,1024]{2,1,0:T(8,128)(2,1)S(1)}, u32[]{:S(2)}, u32[]{:S(2)}) collective-permute-start(bf16[4,16,1024]{2,1,0:T(8,128)(2,1)S(1)} %slice.139), channel_id=1, source_target_pairs={{0,2},{2,4},{4,6},{6,0},{1,3},{3,5},{5,7},{7,1},{8,10},{10,12},{12... | collective-permute-start | bytes 393224 | tf_op jit(solution)/shard_map/ppermute | solution.py:16
  127.7 9.9 %collective-permute-start.11 = (bf16[4,16,1024]{2,1,0:T(8,128)(2,1)S(1)}, bf16[4,16,1024]{2,1,0:T(8,128)(2,1)S(1)}, u32[]{:S(2)}, u32[]{:S(2)}) collective-permute-start(bf16[4,16,1024]{2,1,0:T(8,128)(2,1)S(1)} %slice.140), channel_id=1, source_target_pairs={{0,6},{2,0},{4,2},{6,4},{1,7},{3,1},{5,3},{7,5},{8,14},{10,8},{12,... | collective-permute-start | bytes 393224 | tf_op jit(solution)/shard_map/ppermute | solution.py:16
  127.8 6.3 %collective-permute-start.2 = (bf16[4,16,1024]{2,1,0:T(8,128)(2,1)S(1)}, bf16[4,16,1024]{2,1,0:T(8,128)(2,1)S(1)}, u32[]{:S(2)}, u32[]{:S(2)}) collective-permute-start(bf16[4,16,1024]{2,1,0:T(8,128)(2,1)S(1)} %slice.134), channel_id=1, source_target_pairs={{0,1},{1,8},{8,9},{9,0},{2,3},{3,10},{10,11},{11,2},{4,5},{5,12},{... | collective-permute-start | bytes 393224 | tf_op jit(solution)/shard_map/ppermute | solution.py:16
  128.5 5.6 %collective-permute-start.3 = (bf16[4,16,1024]{2,1,0:T(8,128)(2,1)S(1)}, bf16[4,16,1024]{2,1,0:T(8,128)(2,1)S(1)}, u32[]{:S(2)}, u32[]{:S(2)}) collective-permute-start(bf16[4,16,1024]{2,1,0:T(8,128)(2,1)S(1)} %slice.135), channel_id=1, source_target_pairs={{0,9},{1,0},{8,1},{9,8},{2,11},{3,2},{10,3},{11,10},{4,13},{5,4},{... | collective-permute-start | bytes 393224 | tf_op jit(solution)/shard_map/ppermute | solution.py:16
  134.1 24.5 %collective-permute-start.4 = (bf16[8,4,16,1024]{3,2,1,0:T(8,128)(2,1)S(1)}, bf16[8,4,16,1024]{3,2,1,0:T(8,128)(2,1)S(1)}, u32[]{:S(2)}, u32[]{:S(2)}) collective-permute-start(bf16[8,4,16,1024]{3,2,1,0:T(8,128)(2,1)S(1)} %bitcast_dynamic-update-slice_fusion.19), channel_id=1, source_target_pairs={{0,2},{2,4},{4,6},{6,0},{1,3},{3,5},{5,7},{7,1},{8,10},{10,12},{12... | collective-permute-start | bytes 3145736 | tf_op jit(solution)/shard_map/ppermute | solution.py:16
  137.6 24.9 %collective-permute-start.5 = (bf16[8,4,16,1024]{3,2,1,0:T(8,128)(2,1)S(1)}, bf16[8,4,16,1024]{3,2,1,0:T(8,128)(2,1)S(1)}, u32[]{:S(2)}, u32[]{:S(2)}) collective-permute-start(bf16[8,4,16,1024]{3,2,1,0:T(8,128)(2,1)S(1)} %bitcast_dynamic-update-slice_fusion.19), channel_id=1, source_target_pairs={{0,6},{2,0},{4,2},{6,4},{1,7},{3,1},{5,3},{7,5},{8,14},{10,8},{12,... | collective-permute-start | bytes 3145736 | tf_op jit(solution)/shard_map/ppermute | solution.py:16
  137.6 24.9 %collective-permute-start.12 = (bf16[8,4,16,1024]{3,2,1,0:T(8,128)(2,1)S(1)}, bf16[8,4,16,1024]{3,2,1,0:T(8,128)(2,1)S(1)}, u32[]{:S(2)}, u32[]{:S(2)}) collective-permute-start(bf16[8,4,16,1024]{3,2,1,0:T(8,128)(2,1)S(1)} %bitcast_dynamic-update-slice_fusion.18), channel_id=1, source_target_pairs={{0,1},{1,8},{8,9},{9,0},{2,3},{3,10},{10,11},{11,2},{4,5},{5,12},{... | collective-permute-start | bytes 3145736 | tf_op jit(solution)/shard_map/ppermute | solution.py:16
  137.7 25.0 %collective-permute-start.13 = (bf16[8,4,16,1024]{3,2,1,0:T(8,128)(2,1)S(1)}, bf16[8,4,16,1024]{3,2,1,0:T(8,128)(2,1)S(1)}, u32[]{:S(2)}, u32[]{:S(2)}) collective-permute-start(bf16[8,4,16,1024]{3,2,1,0:T(8,128)(2,1)S(1)} %bitcast_dynamic-update-slice_fusion.18), channel_id=1, source_target_pairs={{0,9},{1,0},{8,1},{9,8},{2,11},{3,2},{10,3},{11,10},{4,13},{5,4},{... | collective-permute-start | bytes 3145736 | tf_op jit(solution)/shard_map/ppermute | solution.py:16
  158.7 12.8 %collective-permute-start.6 = (bf16[4,4,16,1024]{3,2,1,0:T(8,128)(2,1)S(1)}, bf16[4,4,16,1024]{3,2,1,0:T(8,128)(2,1)S(1)}, u32[]{:S(2)}, u32[]{:S(2)}) collective-permute-start(bf16[4,4,16,1024]{3,2,1,0:T(8,128)(2,1)S(1)} %slice.136), channel_id=1, source_target_pairs={{0,2},{2,4},{4,6},{6,0},{1,3},{3,5},{5,7},{7,1},{8,10},{10,12},{12... | collective-permute-start | bytes 1572872 | tf_op jit(solution)/shard_map/ppermute | solution.py:16
  162.5 12.5 %collective-permute-start.7 = (bf16[4,4,16,1024]{3,2,1,0:T(8,128)(2,1)S(1)}, bf16[4,4,16,1024]{3,2,1,0:T(8,128)(2,1)S(1)}, u32[]{:S(2)}, u32[]{:S(2)}) collective-permute-start(bf16[4,4,16,1024]{3,2,1,0:T(8,128)(2,1)S(1)} %slice.137), channel_id=1, source_target_pairs={{0,6},{2,0},{4,2},{6,4},{1,7},{3,1},{5,3},{7,5},{8,14},{10,8},{12,... | collective-permute-start | bytes 1572872 | tf_op jit(solution)/shard_map/ppermute | solution.py:16
  162.7 16.5 %collective-permute-start.14 = (bf16[4,4,16,1024]{3,2,1,0:T(8,128)(2,1)S(1)}, bf16[4,4,16,1024]{3,2,1,0:T(8,128)(2,1)S(1)}, u32[]{:S(2)}, u32[]{:S(2)}) collective-permute-start(bf16[4,4,16,1024]{3,2,1,0:T(8,128)(2,1)S(1)} %slice.141), channel_id=1, source_target_pairs={{0,1},{1,8},{8,9},{9,0},{2,3},{3,10},{10,11},{11,2},{4,5},{5,12},{... | collective-permute-start | bytes 1572872 | tf_op jit(solution)/shard_map/ppermute | solution.py:16
  162.8 17.2 %collective-permute-start.15 = (bf16[4,4,16,1024]{3,2,1,0:T(8,128)(2,1)S(1)}, bf16[4,4,16,1024]{3,2,1,0:T(8,128)(2,1)S(1)}, u32[]{:S(2)}, u32[]{:S(2)}) collective-permute-start(bf16[4,4,16,1024]{3,2,1,0:T(8,128)(2,1)S(1)} %slice.142), channel_id=1, source_target_pairs={{0,9},{1,0},{8,1},{9,8},{2,11},{3,2},{10,3},{11,10},{4,13},{5,4},{... | collective-permute-start | bytes 1572872 | tf_op jit(solution)/shard_map/ppermute | solution.py:16
Sparse Core Ops, SparseCore 0:
  115.9 52.0 all-gather.2

commit v2 on v1

v2 whole, which is shorter than its diff:
```python
import jax
import jax.numpy as jnp
from jax import lax
from jax.experimental import pallas as pl
from jax.experimental.pallas import tpu as pltpu
from jax.sharding import Mesh, PartitionSpec as P

ATTRS = 8
PROFILES = 256

ROW = ("z", "k")
COL = ("xh", "y")
PLANE = ("xh", "y", "xl")
X = ("xh", "xl")


def shift(x, axis, n, by):
    return lax.ppermute(x, axis, [(i, (i + by) % n) for i in range(n)])


def triple(x):
    high = lax.reduce_precision(x, 8, 7)
    rest = x - high
    middle = lax.reduce_precision(rest, 8, 7)
    return high, middle, rest - middle


def around(x, axis):
    return shift(x, axis, 4, 1), shift(x, axis, 4, -1), shift(x, axis, 4, 2)


def other_core(x):
    return lax.ppermute(x, "k", [(0, 1), (1, 0)])


def neighbours(x, axis):
    return shift(x, axis, 4, 1), shift(x, axis, 4, -1)


def across(before, after, axis):
    half = before.shape[0] // 2
    return shift(before[:half], axis, 4, 1), shift(after[half:], axis, 4, -1)


def gram_kernel(upper, lower, columns, out, left):
    step = pl.program_id(0)
    for at in range(4):
        three, far = ((upper[:3], upper[3 + at]) if at < 2 else (lower[:3], lower[3 + at - 2]))

        @pl.when(step == at)
        def _():
            for i, piece in enumerate(tuple(three) + (far,)):
                if at < 2:
                    left[:, i] = piece[...]
                else:
                    left[:, :, i] = piece[...]

    term = lax.dot_general(
        left[...].reshape(columns.shape), columns[...], (((0,), (0,)), ((), ())), preferred_element_type=jnp.float32
    )

    @pl.when(step == 0)
    def _():
        out[...] = term

    @pl.when(step > 0)
    def _():
        out[...] += term


def gram(upper, lower, columns):
    learners, items = columns.shape
    rows = upper[0].shape[2]
    steps = 4
    block = (learners // steps // (16 * rows), 4, rows, items)
    pair = [
        pl.BlockSpec(block, lambda j: (jnp.minimum(j, 1), 0, 0, 0)),
        pl.BlockSpec(block, lambda j: (jnp.maximum(j - 2, 0), 0, 0, 0)),
    ]
    far = pl.BlockSpec(block, lambda j: (0, 0, 0, 0))
    return pl.pallas_call(
        lambda *refs: gram_kernel(refs[:5], refs[5:10], *refs[10:]),
        grid=(steps,),
        in_specs=[pair[0]] * 3 + [far] * 2 + [pair[1]] * 3 + [far] * 2
        + [pl.BlockSpec((learners // steps, items), lambda j: (j, 0))],
        out_specs=pl.BlockSpec((items, items), lambda j: (0, 0)),
        out_shape=jax.ShapeDtypeStruct((items, items), jnp.float32),
        scratch_shapes=[pltpu.VMEM((block[0], 4, 4, rows, items), jnp.bfloat16)],
        compiler_params=pltpu.CompilerParams(
            dimension_semantics=("arbitrary",), vmem_limit_bytes=56 * 2**20
        ),
        name="gram",
    )(*upper, *lower, columns)


def panels(z):
    chunks, rows, items = z.shape
    half = chunks // 2
    x, y = lax.axis_index(X), lax.axis_index("y")

    beside = around(z[:half], X)
    turned, beside = lax.optimization_barrier((swap(z, ROW), beside))
    own = swap(turned, PLANE)
    places = [((y + up) % 4, (x + on) % 4) for up in (0, 3, 1, 2) for on in (0, 3, 1, 2)]
    own = pick(own, [((at // 2) * 4 + up) * 2 + at % 2 for up, at in places]).reshape(16 * rows, items)
    own, beside, z = lax.optimization_barrier((own, beside, z))
    columns = lax.all_gather(own, ROW, tiled=True)

    line = jnp.stack((z[:half],) + beside, axis=1)
    tall = jnp.stack((z[half:],) + around(z[half:], "y"), axis=1)
    near_a = neighbours(line, "y")
    near_b = neighbours(tall, X)
    upper = (line,) + near_a + across(*near_a, "y")
    lower = (tall,) + near_b + across(*near_b, X)
    return gram(upper, lower, columns)


def pick(z, order):
    count, rows, items = z.shape
    source = (jnp.stack(order)[:, None] * rows + jnp.arange(rows)).reshape(-1, 1)
    chosen = (source == jnp.arange(count * rows)).astype(z.dtype)
    taken = jnp.dot(chosen, z.reshape(count * rows, items), preferred_element_type=jnp.float32)
    return taken.astype(z.dtype).reshape(z.shape)


def total(x, axis):
    return jnp.sum(swap(jnp.broadcast_to(x, (16,) + x.shape), axis), axis=0)


def swap(x, axis):
    return lax.all_to_all(x, axis, 0, 0, tiled=True)


def shards(responses, observed, qmatrix, guess, slip):
    learners, items = responses.shape
    cols, rows = 8, 16
    part = learners // cols
    chunk = part // rows

    right = (responses * observed).astype(jnp.bfloat16).reshape(cols, part, items)
    seen = observed.astype(jnp.bfloat16).reshape(cols, part, items)
    table = jnp.concatenate(
        [qmatrix.astype(jnp.float32).T, jnp.stack(triple(guess) + triple(slip)), jnp.zeros((2, items))]
    ).astype(jnp.bfloat16)
    table = jnp.broadcast_to(table, (cols,) + table.shape)
    mixed = swap(jnp.concatenate([right, seen, table], axis=1), COL)
    mixed = mixed.transpose(1, 0, 2).reshape(2 * part + 16, cols * items)
    right, seen, table = mixed[:part], mixed[part : 2 * part], mixed[2 * part :].astype(jnp.float32)
    needs = table[:ATTRS]
    guess = table[8] + table[9] + table[10]
    slip = table[11] + table[12] + table[13]

    codes = jnp.arange(PROFILES, dtype=jnp.int32)
    powers = jnp.arange(ATTRS, dtype=jnp.int32)
    bits = (codes[:, None] >> powers[None, :] & 1).astype(jnp.float32)
    lacking = jnp.dot(1.0 - bits, needs, precision=lax.Precision.HIGHEST)
    prob = jnp.where(lacking == 0.0, 1.0 - slip, guess)
    log0 = jnp.log(1.0 - prob)
    weights = jnp.concatenate([jnp.log(prob) - log0, log0], axis=1)
    data = jnp.concatenate([right, seen], axis=1)
    loglik = sum(
        lax.dot_general(data, w.astype(jnp.bfloat16), (((1,), (1,)), ((), ())), preferred_element_type=jnp.float32)
        for w in triple(weights)
    )
    loglik = loglik.reshape(rows // 2, 2, chunk, PROFILES)
    core = lax.axis_index("k")
    mine = lax.dynamic_index_in_dim(loglik, core, 1, keepdims=False)
    theirs = lax.dynamic_index_in_dim(loglik, 1 - core, 1, keepdims=False)
    loglik = jnp.sum(swap(mine + other_core(theirs), "z"), axis=0)
    posterior = jax.nn.softmax(loglik, axis=1).astype(jnp.bfloat16)
    posterior = swap(jnp.broadcast_to(posterior, (rows, chunk, PROFILES)), ROW).reshape(part, PROFILES)

    expected = jnp.dot(posterior, prob.astype(jnp.bfloat16), preferred_element_type=jnp.float32)
    seen = seen.astype(jnp.float32)
    resid = right.astype(jnp.float32) - seen * expected
    sums = total(jnp.stack([jnp.sum(seen, axis=0), jnp.sum(resid, axis=0), jnp.sum(resid * resid, axis=0)]), PLANE)
    count = jnp.maximum(sums[0], 1.0)
    mean = sums[1] / count
    var = sums[2] / count - mean * mean
    root = jnp.sqrt(jnp.sqrt(jnp.float32(learners * 2)))
    zres = (seen * (resid - mean) * (lax.rsqrt(var + 1e-06) * lax.rsqrt(count) * root)).astype(jnp.bfloat16)
    return panels(zres.reshape(rows, chunk, cols * items))


def solution(mesh):
    named = Mesh(mesh.devices.reshape(8, 2, 2, 4, 2), ("z", "k", "xh", "y", "xl"))
    items = ROW + COL
    placed = (P("xl", items), P("xl", items), P(items, None), P(items), P(items))
    return jax.shard_map(shards, mesh=named, in_specs=placed, out_specs=P(ROW, PLANE), check_vma=False)
```

time: 213 us -> 203 us (0.953)
  blocking collectives: 88.8 us -> 30.5 us
  waiting for transfers between devices: 32.2 us -> 83.7 us
  Pallas kernels: 0 us -> 17.1 us
  local copies, waits for them, and re-layouts: 24.5 us -> 8.44 us
  matrix products: 17.9 us -> 4 us
  starting transfers between devices: 29.9 us -> 38.5 us
    all_to_all x5 -> x2, blocking collectives: 88.8 us -> 30.5 us  [swap(): return lax.all_to_all(x, axis, 0, 0, tiled=True)]
    all_to_all x1 -> x4, waiting for transfers between devices: 8.55 us -> 34.1 us  [swap(): return lax.all_to_all(x, axis, 0, 0, tiled=True)]
    ppermute x16 -> x14, waiting for transfers between devices: 23.6 us -> 48.2 us  [shift(): return lax.ppermute(x, axis, [(i, (i + by) % n) for i in range(n)])]
    pallas_call x0 -> x1, Pallas kernels: none -> 17.1 us  [gram(): pl.pallas_call(lambda *refs: gram_kernel(refs[:5], refs[5:10], *refs[10:]...]
    all_to_all x1 -> x4, starting transfers between devices: 3.51 us -> 20.4 us  [swap(): return lax.all_to_all(x, axis, 0, 0, tiled=True)]
    dot_general x1, matrix products: 15 us -> 1.15 us  [pick(): jnp.dot(chosen, z.reshape(count * rows, items), preferred_element_type=jn...]
    dynamic_update_slice x20 -> x0, local copies, waits for them, and re-layouts: 10.2 us -> none  [place(): return lax.dynamic_update_slice(panel, block, [jnp.int32(s) for s in start])]
    all_gather x1 -> x0, local copies, waits for them, and re-layouts: 8.54 us -> none  [shards(): columns = lax.all_gather(turned, ROW)]
  transfers between devices with their start and end apart: 18 -> 20, of which waited for: 6 -> 14; matrix products, arithmetic and copies ran while one was open for 7% -> 4% of each run, Pallas kernels for 0% -> 0%
where the time goes in v2:
time: 203 us; the launch traced here: 202 us
  waiting for transfers between devices  83.7 us (41%)
  starting transfers between devices  38.5 us (19%)
  blocking collectives  30.5 us (15%)
  Pallas kernels  17.1 us (8%)
  between operations  13.9 us (7%)
  local copies, waits for them, and re-layouts  8.44 us (4%)
  other arithmetic  6.37 us (3%)
  matrix products  4 us (2%)
    ppermute x14, waiting for transfers between devices, shift(): return lax.ppermute(x, axis, [(i, (i + by) % n) for i in range(n)])  48.2 us
    all_to_all x4, waiting for transfers between devices, swap(): return lax.all_to_all(x, axis, 0, 0, tiled=True)  34.1 us
    all_to_all x2, blocking collectives, swap(): return lax.all_to_all(x, axis, 0, 0, tiled=True)  30.5 us
    all_to_all x4, starting transfers between devices, swap(): return lax.all_to_all(x, axis, 0, 0, tiled=True)  20.4 us
    ppermute x14, starting transfers between devices, shift(): return lax.ppermute(x, axis, [(i, (i + by) % n) for i in range(n)])  18 us
    pallas_call x1, Pallas kernels, gram(): pl.pallas_call(lambda *refs: gram_kernel(refs[:5], refs[5:10], *refs[10:]...  17.1 us
  transfers between devices with their start and end apart: 20, of which 14 were waited for; matrix products, arithmetic and copies ran while one was open for 4% of the time, Pallas kernels for 0%

profile of v2, /device:TPU:24, one launch (start us, length us, event | category | flops | bytes accessed | tf_op | source)
XLA Modules:
  0.0 202.4 jit_solution(13009739314940617794)
XLA Ops:
  7.9 2.0 %multiply_convert_fusion = (bf16[2048,128]{1,0:T(8,128)(2,1)S(1)}, bf16[2048,128]{1,0:T(8,128)(2,1)S(1)}) fusion(s32[2048,128]{1,0:T(8,128)} %param.5, s32[2048,128]{1,0:T(8,128)} %param.6), kind=kLoop, calls=%fused_computation.26 | loop fusion | flops 786432 | bytes 3145728 | tf_op jit(solution)/shard_map/convert_element_type | solution.py:140
  11.1 7.1 %all-to-all-start = ((bf16[8,528,128]{2,1,0:T(8,128)(2,1)}), bf16[8,528,128]{2,1,0:T(8,128)(2,1)S(1)}, u32[]{:S(2)}, u32[]{:S(2)}) async-start(bf16[8,528,128]{2,1,0:T(8,128)(2,1)} %pad_maximum_fusion.1), calls=%async_computation | async-start | bytes 2162688 | tf_op jit(solution)/shard_map/all_to_all | solution.py:131
  18.2 14.9 %all-to-all-done = bf16[8,528,128]{2,1,0:T(8,128)(2,1)S(1)} async-done(((bf16[8,528,128]{2,1,0:T(8,128)(2,1)}), bf16[8,528,128]{2,1,0:T(8,128)(2,1)S(1)}, u32[]{:S(2)}, u32[]{:S(2)}) %all-to-all-start) | async-done | bytes 1081376 | tf_op jit(solution)/shard_map/all_to_all | solution.py:131
  36.0 1.3 collective-permute-done
  37.3 17.6 %all_to_all.30 = f32[8,16,256]{2,1,0:T(8,128)S(1)} all-to-all(f32[8,16,256]{2,1,0:T(8,128)S(1)} %bitcast_add_fusion), channel_id=1, replica_groups=mesh['z'=8,'k'=2,'xh'=2,'y'=4,'xl'=2] {'z'}, dimensions={0} | all-to-all | bytes 262144 | tf_op jit(solution)/shard_map/all_to_all | solution.py:131
  56.1 3.5 %all-to-all-start.2 = ((bf16[16,16,256]{2,1,0:T(8,128)(2,1)}), bf16[16,16,256]{2,1,0:T(8,128)(2,1)S(1)}, u32[]{:S(2)}, u32[]{:S(2)}) async-start(bf16[16,16,256]{2,1,0:T(8,128)(2,1)} %broadcast_in_dim.33), calls=%async_computation.2 | async-start | bytes 262144 | tf_op jit(solution)/shard_map/all_to_all | solution.py:131
  59.7 8.6 %all-to-all-done.2 = bf16[16,16,256]{2,1,0:T(8,128)(2,1)S(1)} async-done(((bf16[16,16,256]{2,1,0:T(8,128)(2,1)}), bf16[16,16,256]{2,1,0:T(8,128)(2,1)S(1)}, u32[]{:S(2)}, u32[]{:S(2)}) %all-to-all-start.2) | async-done | bytes 131104 | tf_op jit(solution)/shard_map/all_to_all | solution.py:131
  68.8 12.8 %all_to_all.31 = f32[16,3,1024]{2,1,0:T(4,128)S(1)} all-to-all(f32[16,3,1024]{2,1,0:T(4,128)S(1)} %broadcast_in_dim.34), channel_id=1, replica_groups=mesh['z'=8,'k'=2,'xh'=2,'y'=4,'xl'=2] {'xh','y','xl'}, dimensions={0} | all-to-all | bytes 393216 | tf_op jit(solution)/shard_map/all_to_all | solution.py:131
  82.7 4.2 %all-to-all-start.4 = ((bf16[16,16,1024]{2,1,0:T(8,128)(2,1)}), bf16[16,16,1024]{2,1,0:T(8,128)(2,1)}, u32[]{:S(2)}, u32[]{:S(2)}) async-start(bf16[16,16,1024]{2,1,0:T(8,128)(2,1)} %bitcast.38), calls=%async_computation.4 | async-start | bytes 1048576 | tf_op jit(solution)/shard_map/all_to_all | solution.py:131
  88.0 1.2 collective-permute-start.3
  89.2 1.8 collective-permute-start.2
  91.2 7.5 %collective-permute-done.3 = bf16[8,16,1024]{2,1,0:T(8,128)(2,1)S(1)} collective-permute-done((bf16[8,16,1024]{2,1,0:T(8,128)(2,1)S(1)}, bf16[8,16,1024]{2,1,0:T(8,128)(2,1)S(1)}, u32[]{:S(2)}, u32[]{:S(2)}) %collective-permute-start.3) | collective-permute-done | bytes 262176 | tf_op jit(solution)/shard_map/ppermute | solution.py:18
  98.7 3.1 %collective-permute-done.2 = bf16[8,16,1024]{2,1,0:T(8,128)(2,1)S(1)} collective-permute-done((bf16[8,16,1024]{2,1,0:T(8,128)(2,1)S(1)}, bf16[8,16,1024]{2,1,0:T(8,128)(2,1)S(1)}, u32[]{:S(2)}, u32[]{:S(2)}) %collective-permute-start.2) | collective-permute-done | bytes 262176 | tf_op jit(solution)/shard_map/ppermute | solution.py:18
  101.8 1.8 collective-permute-done.1
  103.6 5.5 %all-to-all-start.5 = ((bf16[16,16,1024]{2,1,0:T(8,128)(2,1)}), bf16[16,16,1024]{2,1,0:T(8,128)(2,1)S(1)}, u32[]{:S(2)}, u32[]{:S(2)}) async-start(bf16[16,16,1024]{2,1,0:T(8,128)(2,1)} %all-to-all-done.4), calls=%async_computation.5 | async-start | bytes 1048576 | tf_op jit(solution)/shard_map/all_to_all | solution.py:131
  109.6 10.6 %all-to-all-done.5 = bf16[16,16,1024]{2,1,0:T(8,128)(2,1)S(1)} async-done(((bf16[16,16,1024]{2,1,0:T(8,128)(2,1)}), bf16[16,16,1024]{2,1,0:T(8,128)(2,1)S(1)}, u32[]{:S(2)}, u32[]{:S(2)}) %all-to-all-start.5) | async-done | bytes 524320 | tf_op jit(solution)/shard_map/all_to_all | solution.py:131
  120.2 1.1 convolution_convert_fusion
  121.4 1.1 slice_bitcast_fusion.5
  122.6 3.2 %collective-permute-start.8 = (bf16[8,16,1024]{2,1,0:T(8,128)(2,1)S(1)}, bf16[8,16,1024]{2,1,0:T(8,128)(2,1)S(1)}, u32[]{:S(2)}, u32[]{:S(2)}) collective-permute-start(bf16[8,16,1024]{2,1,0:T(8,128)(2,1)S(1)} %get-tuple-element.32), channel_id=1, source_target_pairs={{0,2},{2,4},{4,6},{6,0},{1,3},{3,5},{5,7},{7,1},{8,10},{10,12},{12... | collective-permute-start | bytes 786440 | tf_op jit(solution)/shard_map/ppermute | solution.py:18
  126.4 1.5 collective-permute-start.5
  127.9 1.8 collective-permute-start.4
  129.7 8.3 %collective-permute-done.9 = bf16[8,16,1024]{2,1,0:T(8,128)(2,1)S(1)} collective-permute-done((bf16[8,16,1024]{2,1,0:T(8,128)(2,1)S(1)}, bf16[8,16,1024]{2,1,0:T(8,128)(2,1)S(1)}, u32[]{:S(2)}, u32[]{:S(2)}) %collective-permute-start.9) | collective-permute-done | bytes 262176 | tf_op jit(solution)/shard_map/ppermute | solution.py:18
  140.3 1.1 collective-permute-start.11
  141.3 18.7 %collective-permute-done.5 = bf16[8,4,16,1024]{3,2,0,1:T(8,128)(2,1)S(1)} collective-permute-done((bf16[8,4,16,1024]{3,2,0,1:T(8,128)(2,1)S(1)}, bf16[8,4,16,1024]{3,2,0,1:T(8,128)(2,1)S(1)}, u32[]{:S(2)}, u32[]{:S(2)}) %collective-permute-start.5) | collective-permute-done | bytes 1048608 | tf_op jit(solution)/shard_map/ppermute | solution.py:18
  160.2 3.3 %collective-permute-start.6 = (bf16[4,4,16,1024]{3,2,0,1:T(8,128)(2,1)S(1)}, bf16[4,4,16,1024]{3,2,0,1:T(8,128)(2,1)S(1)}, u32[]{:S(2)}, u32[]{:S(2)}) collective-permute-start(bf16[4,4,16,1024]{3,2,0,1:T(8,128)(2,1)S(1)} %slice.119), channel_id=1, source_target_pairs={{0,2},{2,4},{4,6},{6,0},{1,3},{3,5},{5,7},{7,1},{8,10},{10,12},{12... | collective-permute-start | bytes 1572872 | tf_op jit(solution)/shard_map/ppermute | solution.py:18
  163.5 1.6 collective-permute-start.14
  165.8 1.1 copy.42.refs_0_
  166.9 1.1 copy.44.refs_2_
  168.0 1.1 copy.43.refs_1_
  169.0 5.3 %collective-permute-done.7 = bf16[4,4,16,1024]{3,2,0,1:T(8,128)(2,1)S(1)} collective-permute-done((bf16[4,4,16,1024]{3,2,0,1:T(8,128)(2,1)S(1)}, bf16[4,4,16,1024]{3,2,0,1:T(8,128)(2,1)S(1)}, u32[]{:S(2)}, u32[]{:S(2)}) %collective-permute-start.7) | collective-permute-done | bytes 524320 | tf_op jit(solution)/shard_map/ppermute | solution.py:18
  176.2 2.4 %collective-permute-done.13.refs_8_ = bf16[4,4,16,1024]{3,2,1,0:T(8,128)(2,1)} collective-permute-done((bf16[4,4,16,1024]{3,2,1,0:T(8,128)(2,1)S(1)}, bf16[4,4,16,1024]{3,2,1,0:T(8,128)(2,1)}, u32[]{:S(2)}, u32[]{:S(2)}) %collective-permute-start.13) | collective-permute-done | bytes 524320 | tf_op jit(solution)/shard_map/ppermute | solution.py:18
  178.5 17.1 %gram.1 = f32[1024,1024]{1,0:T(8,128)} custom-call(bf16[8,4,16,1024]{3,2,1,0:T(8,128)(2,1)} %copy.42.refs_0_, bf16[8,4,16,1024]{3,2,1,0:T(8,128)(2,1)} %copy.43.refs_1_, bf16[8,4,16,1024]{3,2,1,0:T(8,128)(2,1)} %copy.44.refs_2_, bf16[4,4,16,1024]{3,2,1,0:T(8,128)(2,1)} %copy.45.refs_3_, bf16[4,4,16,1024]{3,2,1,0:T(8,128)(2,1)} %copy.46.refs_4_, ...), custom_call_target="tpu_custom_call" | custom-call | tf_op jit(solution)/shard_map/gram/pallas_call | solution.py:81
  (66 shorter events, 15.1 us)
Async XLA Ops:
  11.1 22.1 %all-to-all-start = ((bf16[8,528,128]{2,1,0:T(8,128)(2,1)}), bf16[8,528,128]{2,1,0:T(8,128)(2,1)S(1)}, u32[]{:S(2)}, u32[]{:S(2)}) async-start(bf16[8,528,128]{2,1,0:T(8,128)(2,1)} %pad_maximum_fusion.1), calls=%async_computation | async-start | bytes 2162688 | tf_op jit(solution)/shard_map/all_to_all | solution.py:131
  35.9 1.4 collective-permute-start
  56.1 12.2 %all-to-all-start.2 = ((bf16[16,16,256]{2,1,0:T(8,128)(2,1)}), bf16[16,16,256]{2,1,0:T(8,128)(2,1)S(1)}, u32[]{:S(2)}, u32[]{:S(2)}) async-start(bf16[16,16,256]{2,1,0:T(8,128)(2,1)} %broadcast_in_dim.33), calls=%async_computation.2 | async-start | bytes 262144 | tf_op jit(solution)/shard_map/all_to_all | solution.py:131
  82.7 20.9 %all-to-all-start.4 = ((bf16[16,16,1024]{2,1,0:T(8,128)(2,1)}), bf16[16,16,1024]{2,1,0:T(8,128)(2,1)}, u32[]{:S(2)}, u32[]{:S(2)}) async-start(bf16[16,16,1024]{2,1,0:T(8,128)(2,1)} %bitcast.38), calls=%async_computation.4 | async-start | bytes 1048576 | tf_op jit(solution)/shard_map/all_to_all | solution.py:131
  88.0 10.8 %collective-permute-start.3 = (bf16[8,16,1024]{2,1,0:T(8,128)(2,1)S(1)}, bf16[8,16,1024]{2,1,0:T(8,128)(2,1)S(1)}, u32[]{:S(2)}, u32[]{:S(2)}) collective-permute-start(bf16[8,16,1024]{2,1,0:T(8,128)(2,1)S(1)} %bitcast.95), channel_id=1, source_target_pairs={{0,8},{1,9},{8,0},{9,1},{2,10},{3,11},{10,2},{11,3},{4,12},{5,13},... | collective-permute-start | bytes 786440 | tf_op jit(solution)/shard_map/ppermute | solution.py:18
  89.2 12.6 %collective-permute-start.2 = (bf16[8,16,1024]{2,1,0:T(8,128)(2,1)S(1)}, bf16[8,16,1024]{2,1,0:T(8,128)(2,1)S(1)}, u32[]{:S(2)}, u32[]{:S(2)}) collective-permute-start(bf16[8,16,1024]{2,1,0:T(8,128)(2,1)S(1)} %bitcast.96), channel_id=1, source_target_pairs={{0,9},{1,0},{8,1},{9,8},{2,11},{3,2},{10,3},{11,10},{4,13},{5,4},{... | collective-permute-start | bytes 786440 | tf_op jit(solution)/shard_map/ppermute | solution.py:18
  91.0 12.6 %collective-permute-start.1 = (bf16[8,16,1024]{2,1,0:T(8,128)(2,1)S(1)}, bf16[8,16,1024]{2,1,0:T(8,128)(2,1)S(1)}, u32[]{:S(2)}, u32[]{:S(2)}) collective-permute-start(bf16[8,16,1024]{2,1,0:T(8,128)(2,1)S(1)} %bitcast.97), channel_id=1, source_target_pairs={{0,1},{1,8},{8,9},{9,0},{2,3},{3,10},{10,11},{11,2},{4,5},{5,12},{... | collective-permute-start | bytes 786440 | tf_op jit(solution)/shard_map/ppermute | solution.py:18
  103.6 16.6 %all-to-all-start.5 = ((bf16[16,16,1024]{2,1,0:T(8,128)(2,1)}), bf16[16,16,1024]{2,1,0:T(8,128)(2,1)S(1)}, u32[]{:S(2)}, u32[]{:S(2)}) async-start(bf16[16,16,1024]{2,1,0:T(8,128)(2,1)} %all-to-all-done.4), calls=%async_computation.5 | async-start | bytes 1048576 | tf_op jit(solution)/shard_map/all_to_all | solution.py:131
  109.1 69.4 %all-gather.2.cloned.1.call-start = ((), (), s32[]{:S(2)}) async-start(), calls=%async_computation.6 | async-start | bytes 8912896 | tf_op jit(solution)/shard_map/all_gather | solution.py:107
  122.5 15.6 %collective-permute-start.9 = (bf16[8,16,1024]{2,1,0:T(8,128)(2,1)S(1)}, bf16[8,16,1024]{2,1,0:T(8,128)(2,1)S(1)}, u32[]{:S(2)}, u32[]{:S(2)}) collective-permute-start(bf16[8,16,1024]{2,1,0:T(8,128)(2,1)S(1)} %get-tuple-element.32), channel_id=1, source_target_pairs={{0,6},{2,0},{4,2},{6,4},{1,7},{3,1},{5,3},{7,5},{8,14},{10,8},{12,... | collective-permute-start | bytes 786440 | tf_op jit(solution)/shard_map/ppermute | solution.py:18
  122.6 15.6 %collective-permute-start.8 = (bf16[8,16,1024]{2,1,0:T(8,128)(2,1)S(1)}, bf16[8,16,1024]{2,1,0:T(8,128)(2,1)S(1)}, u32[]{:S(2)}, u32[]{:S(2)}) collective-permute-start(bf16[8,16,1024]{2,1,0:T(8,128)(2,1)S(1)} %get-tuple-element.32), channel_id=1, source_target_pairs={{0,2},{2,4},{4,6},{6,0},{1,3},{3,5},{5,7},{7,1},{8,10},{10,12},{12... | collective-permute-start | bytes 786440 | tf_op jit(solution)/shard_map/ppermute | solution.py:18
  125.8 13.3 %collective-permute-start.10 = (bf16[8,16,1024]{2,1,0:T(8,128)(2,1)S(1)}, bf16[8,16,1024]{2,1,0:T(8,128)(2,1)S(1)}, u32[]{:S(2)}, u32[]{:S(2)}) collective-permute-start(bf16[8,16,1024]{2,1,0:T(8,128)(2,1)S(1)} %get-tuple-element.32), channel_id=1, source_target_pairs={{0,4},{2,6},{4,0},{6,2},{1,5},{3,7},{5,1},{7,3},{8,12},{10,14},{12... | collective-permute-start | bytes 786440 | tf_op jit(solution)/shard_map/ppermute | solution.py:18
  126.4 33.6 %collective-permute-start.5 = (bf16[8,4,16,1024]{3,2,0,1:T(8,128)(2,1)S(1)}, bf16[8,4,16,1024]{3,2,0,1:T(8,128)(2,1)S(1)}, u32[]{:S(2)}, u32[]{:S(2)}) collective-permute-start(bf16[8,4,16,1024]{3,2,0,1:T(8,128)(2,1)S(1)} %pad_maximum_fusion.2), channel_id=1, source_target_pairs={{0,6},{2,0},{4,2},{6,4},{1,7},{3,1},{5,3},{7,5},{8,14},{10,8},{12,... | collective-permute-start | bytes 3145736 | tf_op jit(solution)/shard_map/ppermute | solution.py:18
  127.9 32.2 %collective-permute-start.4 = (bf16[8,4,16,1024]{3,2,0,1:T(8,128)(2,1)S(1)}, bf16[8,4,16,1024]{3,2,0,1:T(8,128)(2,1)S(1)}, u32[]{:S(2)}, u32[]{:S(2)}) collective-permute-start(bf16[8,4,16,1024]{3,2,0,1:T(8,128)(2,1)S(1)} %pad_maximum_fusion.2), channel_id=1, source_target_pairs={{0,2},{2,4},{4,6},{6,0},{1,3},{3,5},{5,7},{7,1},{8,10},{10,12},{12... | collective-permute-start | bytes 3145736 | tf_op jit(solution)/shard_map/ppermute | solution.py:18
  139.2 26.0 %copy-start = (bf16[8,4,16,1024]{3,2,1,0:T(8,128)(2,1)}, bf16[8,4,16,1024]{3,2,1,0:T(8,128)(2,1)S(1)}, u32[]{:S(2)}) copy-start(bf16[8,4,16,1024]{3,2,1,0:T(8,128)(2,1)S(1)} %pad_maximum_fusion.3.refs_5_) | copy-start | bytes 3145732
  139.2 24.3 %collective-permute-start.12 = (bf16[8,4,16,1024]{3,2,1,0:T(8,128)(2,1)S(1)}, bf16[8,4,16,1024]{3,2,1,0:T(8,128)(2,1)S(1)}, u32[]{:S(2)}, u32[]{:S(2)}) collective-permute-start(bf16[8,4,16,1024]{3,2,1,0:T(8,128)(2,1)S(1)} %pad_maximum_fusion.3.refs_5_), channel_id=1, source_target_pairs={{0,9},{1,0},{8,1},{9,8},{2,11},{3,2},{10,3},{11,10},{4,13},{5,4},{... | collective-permute-start | bytes 3145736 | tf_op jit(solution)/shard_map/ppermute | solution.py:18
  140.3 24.8 %collective-permute-start.11 = (bf16[8,4,16,1024]{3,2,1,0:T(8,128)(2,1)S(1)}, bf16[8,4,16,1024]{3,2,1,0:T(8,128)(2,1)S(1)}, u32[]{:S(2)}, u32[]{:S(2)}) collective-permute-start(bf16[8,4,16,1024]{3,2,1,0:T(8,128)(2,1)S(1)} %pad_maximum_fusion.3.refs_5_), channel_id=1, source_target_pairs={{0,1},{1,8},{8,9},{9,0},{2,3},{3,10},{10,11},{11,2},{4,5},{5,12},{... | collective-permute-start | bytes 3145736 | tf_op jit(solution)/shard_map/ppermute | solution.py:18
  160.1 14.3 %collective-permute-start.7 = (bf16[4,4,16,1024]{3,2,0,1:T(8,128)(2,1)S(1)}, bf16[4,4,16,1024]{3,2,0,1:T(8,128)(2,1)S(1)}, u32[]{:S(2)}, u32[]{:S(2)}) collective-permute-start(bf16[4,4,16,1024]{3,2,0,1:T(8,128)(2,1)S(1)} %slice.120), channel_id=1, source_target_pairs={{0,6},{2,0},{4,2},{6,4},{1,7},{3,1},{5,3},{7,5},{8,14},{10,8},{12,... | collective-permute-start | bytes 1572872 | tf_op jit(solution)/shard_map/ppermute | solution.py:18
  160.2 15.0 %collective-permute-start.6 = (bf16[4,4,16,1024]{3,2,0,1:T(8,128)(2,1)S(1)}, bf16[4,4,16,1024]{3,2,0,1:T(8,128)(2,1)S(1)}, u32[]{:S(2)}, u32[]{:S(2)}) collective-permute-start(bf16[4,4,16,1024]{3,2,0,1:T(8,128)(2,1)S(1)} %slice.119), channel_id=1, source_target_pairs={{0,2},{2,4},{4,6},{6,0},{1,3},{3,5},{5,7},{7,1},{8,10},{10,12},{12... | collective-permute-start | bytes 1572872 | tf_op jit(solution)/shard_map/ppermute | solution.py:18
  163.5 3.4 %copy-start.1 = (bf16[8,4,16,1024]{3,2,1,0:T(8,128)(2,1)}, bf16[8,4,16,1024]{3,2,1,0:T(8,128)(2,1)S(1)}, u32[]{:S(2)}) copy-start(bf16[8,4,16,1024]{3,2,1,0:T(8,128)(2,1)S(1)} %collective-permute-done.12.refs_7_) | copy-start | bytes 3145732
  163.5 12.6 %collective-permute-start.14 = (bf16[4,4,16,1024]{3,2,1,0:T(8,128)(2,1)S(1)}, bf16[4,4,16,1024]{3,2,1,0:T(8,128)(2,1)}, u32[]{:S(2)}, u32[]{:S(2)}) collective-permute-start(bf16[4,4,16,1024]{3,2,1,0:T(8,128)(2,1)S(1)} %slice.122), channel_id=1, source_target_pairs={{0,9},{1,0},{8,1},{9,8},{2,11},{3,2},{10,3},{11,10},{4,13},{5,4},{... | collective-permute-start | bytes 1572872 | tf_op jit(solution)/shard_map/ppermute | solution.py:18
  165.1 2.9 %copy-start.2 = (bf16[8,4,16,1024]{3,2,1,0:T(8,128)(2,1)}, bf16[8,4,16,1024]{3,2,1,0:T(8,128)(2,1)S(1)}, u32[]{:S(2)}) copy-start(bf16[8,4,16,1024]{3,2,1,0:T(8,128)(2,1)S(1)} %collective-permute-done.11.refs_6_) | copy-start | bytes 3145732
  165.2 13.4 %collective-permute-start.13 = (bf16[4,4,16,1024]{3,2,1,0:T(8,128)(2,1)S(1)}, bf16[4,4,16,1024]{3,2,1,0:T(8,128)(2,1)}, u32[]{:S(2)}, u32[]{:S(2)}) collective-permute-start(bf16[4,4,16,1024]{3,2,1,0:T(8,128)(2,1)S(1)} %slice.121), channel_id=1, source_target_pairs={{0,1},{1,8},{8,9},{9,0},{2,3},{3,10},{10,11},{11,2},{4,5},{5,12},{... | collective-permute-start | bytes 1572872 | tf_op jit(solution)/shard_map/ppermute | solution.py:18
Sparse Core Ops, SparseCore 0:
  121.5 54.2 all-gather.1

commit v3 on v2

--- a/solution.py
+++ b/solution.py
@@ -131,19 +131,50 @@
     return lax.all_to_all(x, axis, 0, 0, tiled=True)
 
 
+def pack_kernel(responses, observed, needs, guess, slip, out):
+    parts, part, items = responses.shape
+    for at in range(parts):
+        seen = observed[at]
+        out[at, :part] = (responses[at] * seen).astype(jnp.float32).astype(jnp.bfloat16)
+        out[at, part : 2 * part] = seen.astype(jnp.float32).astype(jnp.bfloat16)
+    row = lax.broadcasted_iota(jnp.int32, (8, items), 0)
+    terms = jnp.zeros((8, items), jnp.float32)
+    for first, value in ((0, guess[...]), (3, slip[...])):
+        for at in range(3):
+            term = value.astype(jnp.bfloat16).astype(jnp.float32)
+            terms = jnp.where(row == first + at, term, terms)
+            value = value - term
+    table = jnp.concatenate([needs[...].astype(jnp.float32), terms], axis=0)
+    for at in range(parts):
+        out[at, 2 * part :] = table.astype(jnp.bfloat16)
+
+
+def packed(responses, observed, qmatrix, guess, slip, cols):
+    learners, items = responses.shape
+    part = learners // cols
+    steps = 2
+    data = pl.BlockSpec((cols // steps, part, items), lambda j: (j, 0, 0))
+    needs = pl.BlockSpec((ATTRS, items), lambda j: (0, 0))
+    line = pl.BlockSpec((1, items), lambda j: (0, 0))
+    rows = 2 * part + 16
+    return pl.pallas_call(
+        pack_kernel,
+        grid=(steps,),
+        in_specs=[data, data, needs, line, line],
+        out_specs=pl.BlockSpec((cols // steps, rows, items), lambda j: (j, 0, 0)),
+        out_shape=jax.ShapeDtypeStruct((cols, rows, items), jnp.bfloat16),
+        compiler_params=pltpu.CompilerParams(dimension_semantics=("arbitrary",)),
+        name="pack",
+    )(responses.reshape(cols, part, items), observed.reshape(cols, part, items), qmatrix.T, guess[None], slip[None])
+
+
 def shards(responses, observed, qmatrix, guess, slip):
     learners, items = responses.shape
     cols, rows = 8, 16
     part = learners // cols
     chunk = part // rows
 
-    right = (responses * observed).astype(jnp.bfloat16).reshape(cols, part, items)
-    seen = observed.astype(jnp.bfloat16).reshape(cols, part, items)
-    table = jnp.concatenate(
-        [qmatrix.astype(jnp.float32).T, jnp.stack(triple(guess) + triple(slip)), jnp.zeros((2, items))]
-    ).astype(jnp.bfloat16)
-    table = jnp.broadcast_to(table, (cols,) + table.shape)
-    mixed = swap(jnp.concatenate([right, seen, table], axis=1), COL)
+    mixed = swap(packed(responses, observed, qmatrix, guess, slip, cols), COL)
     mixed = mixed.transpose(1, 0, 2).reshape(2 * part + 16, cols * items)
     right, seen, table = mixed[:part], mixed[part : 2 * part], mixed[2 * part :].astype(jnp.float32)
     needs = table[:ATTRS]

time: 203 us -> 201 us (level)
  other arithmetic: 6.37 us -> 1.94 us
  Pallas kernels: 17.1 us -> 19.5 us
    pallas_call x0 -> x1, Pallas kernels: none -> 2.45 us  [packed(): pl.pallas_call(pack_kernel, grid=(steps,), in_specs=[data, data, needs, l...]
where the time goes in v3:
time: 201 us
  waiting for transfers between devices  83.3 us (41%)
  starting transfers between devices  38.5 us (19%)
  blocking collectives  30.5 us (15%)
  Pallas kernels  19.5 us (10%)
  between operations  13.9 us (7%)
  local copies, waits for them, and re-layouts  9.07 us (5%)
  matrix products  4.08 us (2%)
    ppermute x14, waiting for transfers between devices, shift(): return lax.ppermute(x, axis, [(i, (i + by) % n) for i in range(n)])  48.2 us
    all_to_all x4, waiting for transfers between devices, swap(): return lax.all_to_all(x, axis, 0, 0, tiled=True)  33.7 us
    all_to_all x2, blocking collectives, swap(): return lax.all_to_all(x, axis, 0, 0, tiled=True)  30.5 us
    all_to_all x4, starting transfers between devices, swap(): return lax.all_to_all(x, axis, 0, 0, tiled=True)  20.4 us
    ppermute x14, starting transfers between devices, shift(): return lax.ppermute(x, axis, [(i, (i + by) % n) for i in range(n)])  18 us
    pallas_call x1, Pallas kernels, gram(): pl.pallas_call(lambda *refs: gram_kernel(refs[:5], refs[5:10], *refs[10:]...  17.1 us
  transfers between devices with their start and end apart: 20, of which 14 were waited for; matrix products, arithmetic and copies ran while one was open for 4% of the time, Pallas kernels for 0%

profile of v3, /device:TPU:24, one launch (start us, length us, event | category | flops | bytes accessed | tf_op | source)
XLA Modules:
  0.0 200.7 jit_solution(10343727063973050003)
XLA Ops:
  6.5 2.4 %pack.1 = bf16[8,528,128]{2,1,0:T(8,128)(2,1)} custom-call(s32[8,256,128]{2,1,0:T(8,128)} %bitcast.76, s32[8,256,128]{2,1,0:T(8,128)} %bitcast.77, s32[8,128]{1,0:T(8,128)} %bitcast.93, f32[1,128]{1,0:T(1,128)} %bitcast.100, f32[1,128]{1,0:T(1,128)} %bitcast.101), custom_call_target="tpu_custom_call" | custom-call | tf_op jit(solution)/shard_map/pack/pallas_call | solution.py:160
  9.0 7.1 %all-to-all-start = ((bf16[8,528,128]{2,1,0:T(8,128)(2,1)}), bf16[8,528,128]{2,1,0:T(8,128)(2,1)S(1)}, u32[]{:S(2)}, u32[]{:S(2)}) async-start(bf16[8,528,128]{2,1,0:T(8,128)(2,1)} %pack.1), calls=%async_computation | async-start | bytes 2162688 | tf_op jit(solution)/shard_map/all_to_all | solution.py:131
  16.1 14.9 %all-to-all-done = bf16[8,528,128]{2,1,0:T(8,128)(2,1)S(1)} async-done(((bf16[8,528,128]{2,1,0:T(8,128)(2,1)}), bf16[8,528,128]{2,1,0:T(8,128)(2,1)S(1)}, u32[]{:S(2)}, u32[]{:S(2)}) %all-to-all-start) | async-done | bytes 1081376 | tf_op jit(solution)/shard_map/all_to_all | solution.py:131
  34.3 1.3 collective-permute-done
  35.6 17.6 %all_to_all.30 = f32[8,16,256]{2,1,0:T(8,128)S(1)} all-to-all(f32[8,16,256]{2,1,0:T(8,128)S(1)} %bitcast_add_fusion), channel_id=1, replica_groups=mesh['z'=8,'k'=2,'xh'=2,'y'=4,'xl'=2] {'z'}, dimensions={0} | all-to-all | bytes 262144 | tf_op jit(solution)/shard_map/all_to_all | solution.py:131
  54.4 3.5 %all-to-all-start.2 = ((bf16[16,16,256]{2,1,0:T(8,128)(2,1)}), bf16[16,16,256]{2,1,0:T(8,128)(2,1)S(1)}, u32[]{:S(2)}, u32[]{:S(2)}) async-start(bf16[16,16,256]{2,1,0:T(8,128)(2,1)} %broadcast_in_dim.33), calls=%async_computation.2 | async-start | bytes 262144 | tf_op jit(solution)/shard_map/all_to_all | solution.py:131
  58.4 8.2 %all-to-all-done.2 = bf16[16,16,256]{2,1,0:T(8,128)(2,1)S(1)} async-done(((bf16[16,16,256]{2,1,0:T(8,128)(2,1)}), bf16[16,16,256]{2,1,0:T(8,128)(2,1)S(1)}, u32[]{:S(2)}, u32[]{:S(2)}) %all-to-all-start.2) | async-done | bytes 131104 | tf_op jit(solution)/shard_map/all_to_all | solution.py:131
  67.1 12.9 %all_to_all.31 = f32[16,3,1024]{2,1,0:T(4,128)S(1)} all-to-all(f32[16,3,1024]{2,1,0:T(4,128)S(1)} %broadcast_in_dim.34), channel_id=1, replica_groups=mesh['z'=8,'k'=2,'xh'=2,'y'=4,'xl'=2] {'xh','y','xl'}, dimensions={0} | all-to-all | bytes 393216 | tf_op jit(solution)/shard_map/all_to_all | solution.py:131
  81.0 4.2 %all-to-all-start.4 = ((bf16[16,16,1024]{2,1,0:T(8,128)(2,1)}), bf16[16,16,1024]{2,1,0:T(8,128)(2,1)}, u32[]{:S(2)}, u32[]{:S(2)}) async-start(bf16[16,16,1024]{2,1,0:T(8,128)(2,1)} %bitcast.36), calls=%async_computation.4 | async-start | bytes 1048576 | tf_op jit(solution)/shard_map/all_to_all | solution.py:131
  86.3 1.2 collective-permute-start.3
  87.5 1.8 collective-permute-start.2
  89.6 7.5 %collective-permute-done.3 = bf16[8,16,1024]{2,1,0:T(8,128)(2,1)S(1)} collective-permute-done((bf16[8,16,1024]{2,1,0:T(8,128)(2,1)S(1)}, bf16[8,16,1024]{2,1,0:T(8,128)(2,1)S(1)}, u32[]{:S(2)}, u32[]{:S(2)}) %collective-permute-start.3) | collective-permute-done | bytes 262176 | tf_op jit(solution)/shard_map/ppermute | solution.py:18
  97.1 3.1 %collective-permute-done.2 = bf16[8,16,1024]{2,1,0:T(8,128)(2,1)S(1)} collective-permute-done((bf16[8,16,1024]{2,1,0:T(8,128)(2,1)S(1)}, bf16[8,16,1024]{2,1,0:T(8,128)(2,1)S(1)}, u32[]{:S(2)}, u32[]{:S(2)}) %collective-permute-start.2) | collective-permute-done | bytes 262176 | tf_op jit(solution)/shard_map/ppermute | solution.py:18
  100.2 1.8 collective-permute-done.1
  101.9 5.5 %all-to-all-start.5 = ((bf16[16,16,1024]{2,1,0:T(8,128)(2,1)}), bf16[16,16,1024]{2,1,0:T(8,128)(2,1)S(1)}, u32[]{:S(2)}, u32[]{:S(2)}) async-start(bf16[16,16,1024]{2,1,0:T(8,128)(2,1)} %all-to-all-done.4), calls=%async_computation.5 | async-start | bytes 1048576 | tf_op jit(solution)/shard_map/all_to_all | solution.py:131
  107.9 10.6 %all-to-all-done.5 = bf16[16,16,1024]{2,1,0:T(8,128)(2,1)S(1)} async-done(((bf16[16,16,1024]{2,1,0:T(8,128)(2,1)}), bf16[16,16,1024]{2,1,0:T(8,128)(2,1)S(1)}, u32[]{:S(2)}, u32[]{:S(2)}) %all-to-all-start.5) | async-done | bytes 524320 | tf_op jit(solution)/shard_map/all_to_all | solution.py:131
  118.5 1.1 convolution_convert_fusion
  119.7 1.1 slice_bitcast_fusion.3
  120.9 3.2 %collective-permute-start.8 = (bf16[8,16,1024]{2,1,0:T(8,128)(2,1)S(1)}, bf16[8,16,1024]{2,1,0:T(8,128)(2,1)S(1)}, u32[]{:S(2)}, u32[]{:S(2)}) collective-permute-start(bf16[8,16,1024]{2,1,0:T(8,128)(2,1)S(1)} %get-tuple-element.30), channel_id=1, source_target_pairs={{0,2},{2,4},{4,6},{6,0},{1,3},{3,5},{5,7},{7,1},{8,10},{10,12},{12... | collective-permute-start | bytes 786440 | tf_op jit(solution)/shard_map/ppermute | solution.py:18
  124.7 1.5 collective-permute-start.5
  126.2 1.8 collective-permute-start.4
  128.0 8.3 %collective-permute-done.9 = bf16[8,16,1024]{2,1,0:T(8,128)(2,1)S(1)} collective-permute-done((bf16[8,16,1024]{2,1,0:T(8,128)(2,1)S(1)}, bf16[8,16,1024]{2,1,0:T(8,128)(2,1)S(1)}, u32[]{:S(2)}, u32[]{:S(2)}) %collective-permute-start.9) | collective-permute-done | bytes 262176 | tf_op jit(solution)/shard_map/ppermute | solution.py:18
  137.5 1.1 collective-permute-start.12
  138.6 1.1 collective-permute-start.11
  139.6 18.7 %collective-permute-done.5 = bf16[8,4,16,1024]{3,2,0,1:T(8,128)(2,1)S(1)} collective-permute-done((bf16[8,4,16,1024]{3,2,0,1:T(8,128)(2,1)S(1)}, bf16[8,4,16,1024]{3,2,0,1:T(8,128)(2,1)S(1)}, u32[]{:S(2)}, u32[]{:S(2)}) %collective-permute-start.5) | collective-permute-done | bytes 1048608 | tf_op jit(solution)/shard_map/ppermute | solution.py:18
  158.5 3.3 %collective-permute-start.6 = (bf16[4,4,16,1024]{3,2,0,1:T(8,128)(2,1)S(1)}, bf16[4,4,16,1024]{3,2,0,1:T(8,128)(2,1)S(1)}, u32[]{:S(2)}, u32[]{:S(2)}) collective-permute-start(bf16[4,4,16,1024]{3,2,0,1:T(8,128)(2,1)S(1)} %slice.119), channel_id=1, source_target_pairs={{0,2},{2,4},{4,6},{6,0},{1,3},{3,5},{5,7},{7,1},{8,10},{10,12},{12... | collective-permute-start | bytes 1572872 | tf_op jit(solution)/shard_map/ppermute | solution.py:18
  161.9 1.5 collective-permute-start.14
  164.1 1.1 copy.46.refs_0_
  165.2 1.1 copy.48.refs_2_
  167.4 5.3 %collective-permute-done.7 = bf16[4,4,16,1024]{3,2,0,1:T(8,128)(2,1)S(1)} collective-permute-done((bf16[4,4,16,1024]{3,2,0,1:T(8,128)(2,1)S(1)}, bf16[4,4,16,1024]{3,2,0,1:T(8,128)(2,1)S(1)}, u32[]{:S(2)}, u32[]{:S(2)}) %collective-permute-start.7) | collective-permute-done | bytes 524320 | tf_op jit(solution)/shard_map/ppermute | solution.py:18
  174.5 2.4 %collective-permute-done.13.refs_8_ = bf16[4,4,16,1024]{3,2,1,0:T(8,128)(2,1)} collective-permute-done((bf16[4,4,16,1024]{3,2,1,0:T(8,128)(2,1)S(1)}, bf16[4,4,16,1024]{3,2,1,0:T(8,128)(2,1)}, u32[]{:S(2)}, u32[]{:S(2)}) %collective-permute-start.13) | collective-permute-done | bytes 524320 | tf_op jit(solution)/shard_map/ppermute | solution.py:18
  176.8 17.1 %gram.1 = f32[1024,1024]{1,0:T(8,128)} custom-call(bf16[8,4,16,1024]{3,2,1,0:T(8,128)(2,1)} %copy.46.refs_0_, bf16[8,4,16,1024]{3,2,1,0:T(8,128)(2,1)} %copy.47.refs_1_, bf16[8,4,16,1024]{3,2,1,0:T(8,128)(2,1)} %copy.48.refs_2_, bf16[4,4,16,1024]{3,2,1,0:T(8,128)(2,1)} %copy.49.refs_3_, bf16[4,4,16,1024]{3,2,1,0:T(8,128)(2,1)} %copy.50.refs_4_, ...), custom_call_target="tpu_custom_call" | custom-call | tf_op jit(solution)/shard_map/gram/pallas_call | solution.py:81
  (62 shorter events, 13.4 us)
Async XLA Ops:
  9.0 22.1 %all-to-all-start = ((bf16[8,528,128]{2,1,0:T(8,128)(2,1)}), bf16[8,528,128]{2,1,0:T(8,128)(2,1)S(1)}, u32[]{:S(2)}, u32[]{:S(2)}) async-start(bf16[8,528,128]{2,1,0:T(8,128)(2,1)} %pack.1), calls=%async_computation | async-start | bytes 2162688 | tf_op jit(solution)/shard_map/all_to_all | solution.py:131
  34.2 1.4 collective-permute-start
  54.4 12.2 %all-to-all-start.2 = ((bf16[16,16,256]{2,1,0:T(8,128)(2,1)}), bf16[16,16,256]{2,1,0:T(8,128)(2,1)S(1)}, u32[]{:S(2)}, u32[]{:S(2)}) async-start(bf16[16,16,256]{2,1,0:T(8,128)(2,1)} %broadcast_in_dim.33), calls=%async_computation.2 | async-start | bytes 262144 | tf_op jit(solution)/shard_map/all_to_all | solution.py:131
  81.0 20.9 %all-to-all-start.4 = ((bf16[16,16,1024]{2,1,0:T(8,128)(2,1)}), bf16[16,16,1024]{2,1,0:T(8,128)(2,1)}, u32[]{:S(2)}, u32[]{:S(2)}) async-start(bf16[16,16,1024]{2,1,0:T(8,128)(2,1)} %bitcast.36), calls=%async_computation.4 | async-start | bytes 1048576 | tf_op jit(solution)/shard_map/all_to_all | solution.py:131
  86.3 10.8 %collective-permute-start.3 = (bf16[8,16,1024]{2,1,0:T(8,128)(2,1)S(1)}, bf16[8,16,1024]{2,1,0:T(8,128)(2,1)S(1)}, u32[]{:S(2)}, u32[]{:S(2)}) collective-permute-start(bf16[8,16,1024]{2,1,0:T(8,128)(2,1)S(1)} %bitcast.80), channel_id=1, source_target_pairs={{0,8},{1,9},{8,0},{9,1},{2,10},{3,11},{10,2},{11,3},{4,12},{5,13},... | collective-permute-start | bytes 786440 | tf_op jit(solution)/shard_map/ppermute | solution.py:18
  87.5 12.6 %collective-permute-start.2 = (bf16[8,16,1024]{2,1,0:T(8,128)(2,1)S(1)}, bf16[8,16,1024]{2,1,0:T(8,128)(2,1)S(1)}, u32[]{:S(2)}, u32[]{:S(2)}) collective-permute-start(bf16[8,16,1024]{2,1,0:T(8,128)(2,1)S(1)} %bitcast.81), channel_id=1, source_target_pairs={{0,9},{1,0},{8,1},{9,8},{2,11},{3,2},{10,3},{11,10},{4,13},{5,4},{... | collective-permute-start | bytes 786440 | tf_op jit(solution)/shard_map/ppermute | solution.py:18
  89.3 12.6 %collective-permute-start.1 = (bf16[8,16,1024]{2,1,0:T(8,128)(2,1)S(1)}, bf16[8,16,1024]{2,1,0:T(8,128)(2,1)S(1)}, u32[]{:S(2)}, u32[]{:S(2)}) collective-permute-start(bf16[8,16,1024]{2,1,0:T(8,128)(2,1)S(1)} %bitcast.82), channel_id=1, source_target_pairs={{0,1},{1,8},{8,9},{9,0},{2,3},{3,10},{10,11},{11,2},{4,5},{5,12},{... | collective-permute-start | bytes 786440 | tf_op jit(solution)/shard_map/ppermute | solution.py:18
  101.9 16.6 %all-to-all-start.5 = ((bf16[16,16,1024]{2,1,0:T(8,128)(2,1)}), bf16[16,16,1024]{2,1,0:T(8,128)(2,1)S(1)}, u32[]{:S(2)}, u32[]{:S(2)}) async-start(bf16[16,16,1024]{2,1,0:T(8,128)(2,1)} %all-to-all-done.4), calls=%async_computation.5 | async-start | bytes 1048576 | tf_op jit(solution)/shard_map/all_to_all | solution.py:131
  107.4 69.4 %all-gather.2.cloned.1.call-start = ((), (), s32[]{:S(2)}) async-start(), calls=%async_computation.6 | async-start | bytes 8912896 | tf_op jit(solution)/shard_map/all_gather | solution.py:107
  120.8 15.6 %collective-permute-start.9 = (bf16[8,16,1024]{2,1,0:T(8,128)(2,1)S(1)}, bf16[8,16,1024]{2,1,0:T(8,128)(2,1)S(1)}, u32[]{:S(2)}, u32[]{:S(2)}) collective-permute-start(bf16[8,16,1024]{2,1,0:T(8,128)(2,1)S(1)} %get-tuple-element.30), channel_id=1, source_target_pairs={{0,6},{2,0},{4,2},{6,4},{1,7},{3,1},{5,3},{7,5},{8,14},{10,8},{12,... | collective-permute-start | bytes 786440 | tf_op jit(solution)/shard_map/ppermute | solution.py:18
  120.9 15.6 %collective-permute-start.8 = (bf16[8,16,1024]{2,1,0:T(8,128)(2,1)S(1)}, bf16[8,16,1024]{2,1,0:T(8,128)(2,1)S(1)}, u32[]{:S(2)}, u32[]{:S(2)}) collective-permute-start(bf16[8,16,1024]{2,1,0:T(8,128)(2,1)S(1)} %get-tuple-element.30), channel_id=1, source_target_pairs={{0,2},{2,4},{4,6},{6,0},{1,3},{3,5},{5,7},{7,1},{8,10},{10,12},{12... | collective-permute-start | bytes 786440 | tf_op jit(solution)/shard_map/ppermute | solution.py:18
  124.1 13.3 %collective-permute-start.10 = (bf16[8,16,1024]{2,1,0:T(8,128)(2,1)S(1)}, bf16[8,16,1024]{2,1,0:T(8,128)(2,1)S(1)}, u32[]{:S(2)}, u32[]{:S(2)}) collective-permute-start(bf16[8,16,1024]{2,1,0:T(8,128)(2,1)S(1)} %get-tuple-element.30), channel_id=1, source_target_pairs={{0,4},{2,6},{4,0},{6,2},{1,5},{3,7},{5,1},{7,3},{8,12},{10,14},{12... | collective-permute-start | bytes 786440 | tf_op jit(solution)/shard_map/ppermute | solution.py:18
  124.7 33.6 %collective-permute-start.5 = (bf16[8,4,16,1024]{3,2,0,1:T(8,128)(2,1)S(1)}, bf16[8,4,16,1024]{3,2,0,1:T(8,128)(2,1)S(1)}, u32[]{:S(2)}, u32[]{:S(2)}) collective-permute-start(bf16[8,4,16,1024]{3,2,0,1:T(8,128)(2,1)S(1)} %pad_maximum_fusion.2), channel_id=1, source_target_pairs={{0,6},{2,0},{4,2},{6,4},{1,7},{3,1},{5,3},{7,5},{8,14},{10,8},{12,... | collective-permute-start | bytes 3145736 | tf_op jit(solution)/shard_map/ppermute | solution.py:18
  126.2 32.2 %collective-permute-start.4 = (bf16[8,4,16,1024]{3,2,0,1:T(8,128)(2,1)S(1)}, bf16[8,4,16,1024]{3,2,0,1:T(8,128)(2,1)S(1)}, u32[]{:S(2)}, u32[]{:S(2)}) collective-permute-start(bf16[8,4,16,1024]{3,2,0,1:T(8,128)(2,1)S(1)} %pad_maximum_fusion.2), channel_id=1, source_target_pairs={{0,2},{2,4},{4,6},{6,0},{1,3},{3,5},{5,7},{7,1},{8,10},{10,12},{12... | collective-permute-start | bytes 3145736 | tf_op jit(solution)/shard_map/ppermute | solution.py:18
  137.5 25.9 %copy-start = (bf16[8,4,16,1024]{3,2,1,0:T(8,128)(2,1)}, bf16[8,4,16,1024]{3,2,1,0:T(8,128)(2,1)S(1)}, u32[]{:S(2)}) copy-start(bf16[8,4,16,1024]{3,2,1,0:T(8,128)(2,1)S(1)} %pad_maximum_fusion.3.refs_5_) | copy-start | bytes 3145732
  137.5 24.3 %collective-permute-start.12 = (bf16[8,4,16,1024]{3,2,1,0:T(8,128)(2,1)S(1)}, bf16[8,4,16,1024]{3,2,1,0:T(8,128)(2,1)S(1)}, u32[]{:S(2)}, u32[]{:S(2)}) collective-permute-start(bf16[8,4,16,1024]{3,2,1,0:T(8,128)(2,1)S(1)} %pad_maximum_fusion.3.refs_5_), channel_id=1, source_target_pairs={{0,9},{1,0},{8,1},{9,8},{2,11},{3,2},{10,3},{11,10},{4,13},{5,4},{... | collective-permute-start | bytes 3145736 | tf_op jit(solution)/shard_map/ppermute | solution.py:18
  138.6 24.8 %collective-permute-start.11 = (bf16[8,4,16,1024]{3,2,1,0:T(8,128)(2,1)S(1)}, bf16[8,4,16,1024]{3,2,1,0:T(8,128)(2,1)S(1)}, u32[]{:S(2)}, u32[]{:S(2)}) collective-permute-start(bf16[8,4,16,1024]{3,2,1,0:T(8,128)(2,1)S(1)} %pad_maximum_fusion.3.refs_5_), channel_id=1, source_target_pairs={{0,1},{1,8},{8,9},{9,0},{2,3},{3,10},{10,11},{11,2},{4,5},{5,12},{... | collective-permute-start | bytes 3145736 | tf_op jit(solution)/shard_map/ppermute | solution.py:18
  158.4 14.3 %collective-permute-start.7 = (bf16[4,4,16,1024]{3,2,0,1:T(8,128)(2,1)S(1)}, bf16[4,4,16,1024]{3,2,0,1:T(8,128)(2,1)S(1)}, u32[]{:S(2)}, u32[]{:S(2)}) collective-permute-start(bf16[4,4,16,1024]{3,2,0,1:T(8,128)(2,1)S(1)} %slice.120), channel_id=1, source_target_pairs={{0,6},{2,0},{4,2},{6,4},{1,7},{3,1},{5,3},{7,5},{8,14},{10,8},{12,... | collective-permute-start | bytes 1572872 | tf_op jit(solution)/shard_map/ppermute | solution.py:18
  158.5 15.0 %collective-permute-start.6 = (bf16[4,4,16,1024]{3,2,0,1:T(8,128)(2,1)S(1)}, bf16[4,4,16,1024]{3,2,0,1:T(8,128)(2,1)S(1)}, u32[]{:S(2)}, u32[]{:S(2)}) collective-permute-start(bf16[4,4,16,1024]{3,2,0,1:T(8,128)(2,1)S(1)} %slice.119), channel_id=1, source_target_pairs={{0,2},{2,4},{4,6},{6,0},{1,3},{3,5},{5,7},{7,1},{8,10},{10,12},{12... | collective-permute-start | bytes 1572872 | tf_op jit(solution)/shard_map/ppermute | solution.py:18
  161.8 4.5 %copy-start.1 = (bf16[8,4,16,1024]{3,2,1,0:T(8,128)(2,1)}, bf16[8,4,16,1024]{3,2,1,0:T(8,128)(2,1)S(1)}, u32[]{:S(2)}) copy-start(bf16[8,4,16,1024]{3,2,1,0:T(8,128)(2,1)S(1)} %collective-permute-done.12.refs_7_) | copy-start | bytes 3145732
  161.9 12.6 %collective-permute-start.14 = (bf16[4,4,16,1024]{3,2,1,0:T(8,128)(2,1)S(1)}, bf16[4,4,16,1024]{3,2,1,0:T(8,128)(2,1)}, u32[]{:S(2)}, u32[]{:S(2)}) collective-permute-start(bf16[4,4,16,1024]{3,2,1,0:T(8,128)(2,1)S(1)} %slice.122), channel_id=1, source_target_pairs={{0,9},{1,0},{8,1},{9,8},{2,11},{3,2},{10,3},{11,10},{4,13},{5,4},{... | collective-permute-start | bytes 1572872 | tf_op jit(solution)/shard_map/ppermute | solution.py:18
  163.4 2.9 %copy-start.2 = (bf16[8,4,16,1024]{3,2,1,0:T(8,128)(2,1)}, bf16[8,4,16,1024]{3,2,1,0:T(8,128)(2,1)S(1)}, u32[]{:S(2)}) copy-start(bf16[8,4,16,1024]{3,2,1,0:T(8,128)(2,1)S(1)} %collective-permute-done.11.refs_6_) | copy-start | bytes 3145732
  163.5 13.4 %collective-permute-start.13 = (bf16[4,4,16,1024]{3,2,1,0:T(8,128)(2,1)S(1)}, bf16[4,4,16,1024]{3,2,1,0:T(8,128)(2,1)}, u32[]{:S(2)}, u32[]{:S(2)}) collective-permute-start(bf16[4,4,16,1024]{3,2,1,0:T(8,128)(2,1)S(1)} %slice.121), channel_id=1, source_target_pairs={{0,1},{1,8},{8,9},{9,0},{2,3},{3,10},{10,11},{11,2},{4,5},{5,12},{... | collective-permute-start | bytes 1572872 | tf_op jit(solution)/shard_map/ppermute | solution.py:18
Sparse Core Ops, SparseCore 0:
  119.8 54.2 all-gather.1
